TPU v7x, 32 devices: a whole 2x2x4 slice. The times are simulated.
32 devices in a mesh: req: 4 (over z), head: 2 (over core), exp: 4 (over y, x).
Axes of the slice: x: 2, y: 2, z: 4, core: 2. Of those that a mesh axis runs over, the one named last changes fastest.
Arguments:
- queries: bfloat16 [64, 64, 128], P(('req', 'exp'), 'head'), may hold values from -18 to 18
- keys: bfloat16 [64, 512, 4, 128], P(('req', 'exp'), None, 'head'), may hold values from -15 to 15
- values: bfloat16 [64, 512, 4, 128], P(('req', 'exp'), None, 'head'), may hold values from -12 to 12
- lengths: int32 [64], P(('req', 'exp')), may hold values from 1 to 512, as said below
- out_weight: bfloat16 [8192, 4096], P('head', 'exp'), may hold values from -0.0625 to 0.0625
- resid: bfloat16 [64, 4096], P('req', 'exp'), may hold values from -11 to 11
- norm_gain: float32 [4096], replicated, may hold values from 0.25 to 1.75
- expert_ids: int32 [64, 8], P('req'), may hold values from 0 to 15, all different within a row; in each aligned block of 16 rows (0 to 15, 16 to 31, ...) at most 8 rows name the same one
- route_weights: float32 [64, 8], P('req'), may hold values from 0.1 to 1
- w_gate: bfloat16 [16, 4096, 768], P(('req', 'exp'), None, 'head'), may hold values from -0.09375 to 0.09375
- w_up: bfloat16 [16, 4096, 768], P(('req', 'exp'), None, 'head'), may hold values from -0.09375 to 0.09375
- w_down: bfloat16 [16, 768, 4096], P(('req', 'exp'), 'head'), may hold values from -0.21875 to 0.21875
Outputs:
- layer_out: bfloat16 [64, 4096], P('req', 'exp')
Inputs may be any that keep to these rules, and one draw needn't show every extreme that they name: `expert_ids`: within each aligned block of 16 rows (the tokens of one index of req), a row names 8 different experts and no expert is named by more than 8 rows; some expert is named by exactly 8 rows. `lengths`: some question's cache is full.
All inputs are finite; a program needn't handle non-finite values.
Results may differ from a plain program's by a relative error of at most 0.0049.
Values may be sent and summed in bfloat16 or wider, within the bound.
No kernel may reach another device: no remote copies, remote signals or barrier semaphores. Data moves between devices by JAX's collectives and lax.ppermute only.
A program may use at most 64 MiB of HBM per device.

v0:
```python
import math

import jax
import jax.numpy as jnp
from jax import lax
from jax.sharding import PartitionSpec as P


def local(
    queries,
    keys,
    values,
    lengths,
    out_weight,
    resid,
    norm_gain,
    expert_ids,
    route_weights,
    w_gate,
    w_up,
    w_down,
):
    req_count = lax.axis_size("req")
    exp_count = lax.axis_size("exp")
    column = lax.axis_index("exp")
    rows_dev, heads_dev, head_size = queries.shape
    slots = keys.shape[1]
    kv_heads = keys.shape[2]
    group_rows, col_width = resid.shape
    full_width = norm_gain.shape[0]
    capacity = 2 * rows_dev
    expert_total = req_count * exp_count
    grouped_result = queries.reshape(rows_dev, kv_heads, heads_dev // kv_heads, head_size)
    logits = jnp.einsum(
        "rgjd,rcgd->rgjc", grouped_result, keys, preferred_element_type=jnp.float32
    ) * (1.0 / math.sqrt(head_size))
    visible = jnp.arange(slots, dtype=jnp.int32)[None, :] < lengths[:, None]
    logits = jnp.where(visible[:, None, None, :], logits, -1e30)
    peak = jnp.max(logits, axis=-1, keepdims=True)
    raised = jnp.exp(logits - peak)
    soft_weights = (raised / jnp.sum(raised, axis=-1, keepdims=True)).astype(jnp.bfloat16)
    attended = jnp.einsum(
        "rgjc,rcgd->rgjd", soft_weights, values, preferred_element_type=jnp.float32
    )
    attended = attended.reshape(rows_dev, heads_dev * head_size).astype(jnp.bfloat16)
    projected = jnp.dot(
        lax.all_gather(attended, "exp", axis=0, tiled=True),
        out_weight,
        preferred_element_type=jnp.float32,
    )
    projected = lax.psum(projected, "head")
    hidden = resid.astype(jnp.float32) + projected
    squares = lax.psum(jnp.sum(hidden * hidden, axis=1), "exp")
    inverse = lax.rsqrt(squares / full_width + 1e-06)
    gain_cols = lax.dynamic_slice_in_dim(norm_gain, column * col_width, col_width)
    normed_cols = (hidden * inverse[:, None] * gain_cols[None, :]).astype(jnp.bfloat16)
    matched = expert_ids[:, :, None] == jnp.arange(expert_total, dtype=jnp.int32)[None, None, :]
    chosen = jnp.any(matched, axis=1)
    weighting = jnp.sum(jnp.where(matched, route_weights[:, :, None], 0.0), axis=1)
    position = jnp.cumsum(chosen.astype(jnp.int32), axis=0) - 1
    selector = (
        position.T[:, None, :] == jnp.arange(capacity, dtype=jnp.int32)[None, :, None]
    ) & chosen.T[:, None, :]
    spread = jnp.where(selector, weighting.T[:, None, :], 0.0)
    outgoing = jnp.einsum(
        "ecg,gd->ecd",
        selector.astype(jnp.bfloat16),
        normed_cols,
        preferred_element_type=jnp.float32,
    ).astype(jnp.bfloat16)
    arrived = lax.all_to_all(outgoing, ("req", "exp"), split_axis=0, concat_axis=0, tiled=True)
    items = arrived.shape[1]
    rows = arrived.reshape(req_count, exp_count, items, col_width).transpose(0, 2, 1, 3)
    rows = rows.reshape(req_count, items, exp_count * col_width)
    gate_act = jnp.einsum("snd,df->snf", rows, w_gate[0], preferred_element_type=jnp.float32)
    up_act = jnp.einsum("snd,df->snf", rows, w_up[0], preferred_element_type=jnp.float32)
    activated = (jax.nn.silu(gate_act) * up_act).astype(jnp.bfloat16)
    expert_out = jnp.einsum("snf,fd->snd", activated, w_down[0], preferred_element_type=jnp.float32)
    expert_out = lax.psum(expert_out, "head")
    pieces = expert_out.reshape(req_count, items, exp_count, col_width).transpose(0, 2, 1, 3)
    pieces = pieces.reshape(req_count * exp_count, items, col_width)
    returned = lax.all_to_all(pieces, ("req", "exp"), split_axis=0, concat_axis=0, tiled=True)
    mixture = jnp.einsum("ecg,ecd->gd", spread, returned, precision=lax.Precision.HIGHEST)
    return (hidden + mixture).astype(jnp.bfloat16)


def solution(mesh):
    in_specs = (
        P(("req", "exp"), "head", None),
        P(("req", "exp"), None, "head", None),
        P(("req", "exp"), None, "head", None),
        P(("req", "exp")),
        P("head", "exp"),
        P("req", "exp"),
        P(),
        P("req", None),
        P("req", None),
        P(("req", "exp"), None, "head"),
        P(("req", "exp"), None, "head"),
        P(("req", "exp"), "head", None),
    )
    out_specs = P("req", "exp")
    return jax.shard_map(local, mesh=mesh, in_specs=in_specs, out_specs=out_specs, check_vma=False)
```

profile of v0, /device:TPU:0, one launch (start us, length us, event | category | flops | bytes accessed | tf_op | source)
XLA Modules:
  0.0 127.2 jit_solution(6337636310465268059)
XLA Ops:
  6.5 0.0 copy-start
  6.5 0.0 all-reduce.3.cloned.1.call-start
  6.5 0.9 iota_compare_fusion.2
  7.4 1.7 %fusion.9 = f32[4,2,16,512]{3,2,1,0:T(8,128)S(1)} fusion(bf16[4,2,16,128]{3,2,1,0:T(8,128)(2,1)} %bitcast.52, bf16[4,512,2,128]{3,2,1,0:T(2,128)(2,1)} %param.13, pred[4,512]{1,0:T(4,128)(4,1)S(1)} %iota_compare_fusion.2), kind=kOutput, calls=%fused_computation.11 | convolution fusion | flops 16908288 | bytes 1345536 | tf_op jit(solution)/shard_map/rgjd,rcgd->rgjc/dot_general | solution.py:34
  9.1 0.2 fusion.44
  9.3 1.5 %convolution_convert_fusion.1 = bf16[4,2,16,128]{3,2,1,0:T(8,128)(2,1)S(1)} fusion(bf16[4,512,2,128]{3,2,1,0:T(2,128)(2,1)} %param.14, f32[4,2,16]{2,1,0:T(2,128)S(1)} %fusion.44, f32[4,2,16,512]{3,2,1,0:T(8,128)S(1)} %fusion.9), kind=kOutput, calls=%fused_computation.16 | convolution fusion | flops 16990848 | bytes 1344000 | tf_op jit(solution)/shard_map/rgjc,rcgd->rgjd/dot_general | solution.py:42
  10.9 9.9 %all-gather = bf16[4,4,4096]{2,1,0:T(4,128)(2,1)S(1)} all-gather(bf16[1,4,4096]{2,1,0:T(4,128)(2,1)S(1)} %reshape.45), channel_id=1, replica_groups=mesh['req'=4,'head'=2,'exp'=4] {'exp'}, dimensions={0}, use_global_device_ids=true | all-gather | bytes 163840 | tf_op jit(solution)/shard_map/all_gather | solution.py:47
  20.9 0.0 copy-start.3
  20.9 0.0 copy-start.2
  20.9 5.2 %fusion.45 = f32[16,1024]{1,0:T(8,128)} fusion(bf16[16,4096]{1,0:T(8,128)(2,1)S(1)} %reshape.46, bf16[4096,1024]{1,0:T(8,128)(2,1)} %param.16), kind=kOutput, calls=%fused_computation.52 | convolution fusion | flops 134217728 | bytes 8585216 | tf_op jit(solution)/shard_map/dot_general | solution.py:46
  26.1 0.0 all-reduce.3.cloned.1.call-update
  26.1 0.0 all-reduce.5.cloned.1.call-start
  26.2 0.1 copy.19
  26.4 0.1 copy.20
  26.5 0.1 copy.22
  26.6 17.7 %all-reduce.3.cloned.1.call-done = f32[16,1024]{1,0:T(8,128)} async-done(((f32[16,1024]{1,0:T(8,128)}), f32[16,1024]{1,0:T(8,128)}) %all-reduce.3.cloned.1.call-update) | async-done | bytes 65552 | tf_op jit(solution)/shard_map/psum | solution.py:51
  44.3 1.0 multiply_reduce_fusion
  45.3 0.7 dynamic_slice.3
  46.0 10.1 %psum.22 = f32[16]{0:T(128)S(1)} all-reduce(f32[16]{0:T(128)S(1)} %multiply_reduce_fusion), channel_id=1, replica_groups=mesh['req'=4,'head'=2,'exp'=4] {'exp'}, use_global_device_ids=true, to_apply=%region_7.8 | all-reduce | flops 16 | bytes 128 | tf_op jit(solution)/shard_map/psum | solution.py:53
  56.1 1.1 convolution_convert_fusion
  57.2 13.0 %all_to_all.10 = bf16[16,8,1024]{2,1,0:T(8,128)(2,1)S(1)} all-to-all(bf16[16,8,1024]{2,1,0:T(8,128)(2,1)S(1)} %convolution_convert_fusion), channel_id=1, replica_groups=mesh['req'=4,'head'=2,'exp'=4] {'req','exp'}, dimensions={0} | all-to-all | bytes 524288 | tf_op jit(solution)/shard_map/all_to_all | solution.py:71
  70.2 2.4 %fusion.5 = f32[4,8,384]{2,1,0:T(8,128)S(1)} fusion(bf16[4,8,4096]{2,1,0:T(8,128)(2,1)S(1)} %bitcast.48, bf16[1,4096,384]{2,1,0:T(8,128)(2,1)} %param.21), kind=kOutput, calls=%fused_computation.5 | convolution fusion | flops 100663296 | bytes 3457024 | tf_op jit(solution)/shard_map/snd,df->snf/dot_general | solution.py:75
  72.7 4.1 %fusion.1 = f32[4,8,4096]{2,1,0:T(8,128)} fusion(bf16[1,384,4096]{2,1,0:T(8,128)(2,1)S(1)} %copy-done, bf16[4,8,4096]{2,1,0:T(8,128)(2,1)S(1)} %bitcast.49, bf16[1,4096,384]{2,1,0:T(8,128)(2,1)} %param.22, f32[4,8,384]{2,1,0:T(8,128)S(1)} %fusion.5), kind=kOutput, calls=%fused_computation.1 | convolution fusion | flops 201400320 | bytes 7127040 | tf_op jit(solution)/shard_map/snf,fd->snd/dot_general | solution.py:78
  76.8 0.0 all-reduce.5.cloned.1.call-update
  76.8 16.7 %all-reduce.5.cloned.1.call-done = f32[4,8,4096]{2,1,0:T(8,128)} async-done(((f32[4,8,4096]{2,1,0:T(8,128)}), f32[4,8,4096]{2,1,0:T(8,128)}) %all-reduce.5.cloned.1.call-update) | async-done | bytes 524304 | tf_op jit(solution)/shard_map/psum | solution.py:79
  93.4 1.1 fusion.43
  94.6 0.8 pad_maximum_fusion
  95.4 6.9 %all-to-all-start.1 = ((f32[16,8,1024]{2,1,0:T(8,128)}), f32[16,8,1024]{2,1,0:T(8,128)}, u32[]{:S(2)}, u32[]{:S(2)}) async-start(f32[16,8,1024]{2,1,0:T(8,128)} %bitcast.50), calls=%async_computation.1 | async-start | bytes 1048576 | tf_op jit(solution)/shard_map/all_to_all | solution.py:82
  102.3 0.0 copy-done.4
  102.3 0.1 copy.21
  102.4 15.4 %all-to-all-done.1 = f32[16,8,1024]{2,1,0:T(8,128)} async-done(((f32[16,8,1024]{2,1,0:T(8,128)}), f32[16,8,1024]{2,1,0:T(8,128)}, u32[]{:S(2)}, u32[]{:S(2)}) %all-to-all-start.1) | async-done | bytes 524320 | tf_op jit(solution)/shard_map/all_to_all | solution.py:82
  117.9 2.5 %fusion.14 = bf16[16,1024]{1,0:T(8,128)(2,1)} fusion(f32[16,8,1024]{2,1,0:T(8,128)} %all-to-all-done.1, f32[16,16]{0,1:T(8,128)S(1)} %copy.21, f32[16,1024]{1,0:T(8,128)S(1)} %copy-done.1, bf16[16,1024]{1,0:T(8,128)(2,1)S(1)} %copy-done.2, s32[16,16]{0,1:T(8,128)S(1)} %add_bitcast_fusion, pred[16,16]{0,1:T(8,128)(4,1)S(1)} %copy.20), kind=kOutput, calls=%fused_computation.15 | convolution fusion | flops 25237504 | bytes 657664 | tf_op jit(solution)/shard_map/ecg,ecd->gd/dot_general | solution.py:83
  (15 shorter events, 0.2 us)
Async XLA Ops:
  6.5 66.1 %copy-start = (bf16[1,384,4096]{2,1,0:T(8,128)(2,1)S(1)}, bf16[1,384,4096]{2,1,0:T(8,128)(2,1)}, u32[]{:S(2)}) copy-start(bf16[1,384,4096]{2,1,0:T(8,128)(2,1)} %param.23) | copy-start | bytes 9437188
  6.5 37.8 %all-reduce.3.cloned.1.call-start = ((), (), s32[]{:S(2)}) async-start(), calls=%async_computation.2 | async-start | bytes 131072 | tf_op jit(solution)/shard_map/psum | solution.py:51
  20.9 5.3 %copy-start.3 = (s32[16,8]{0,1:T(8,128)S(1)}, s32[16,8]{0,1:T(8,128)}, u32[]{:S(2)}) copy-start(s32[16,8]{0,1:T(8,128)} %param.19) | copy-start | bytes 1540
  20.9 23.4 %copy-start.2 = (bf16[16,1024]{1,0:T(8,128)(2,1)S(1)}, bf16[16,1024]{1,0:T(8,128)(2,1)}, u32[]{:S(2)}) copy-start(bf16[16,1024]{1,0:T(8,128)(2,1)} %param.17) | copy-start | bytes 98308
  26.1 67.3 %all-reduce.5.cloned.1.call-start = ((), (), s32[]{:S(2)}) async-start(), calls=%async_computation.3 | async-start | bytes 1048576 | tf_op jit(solution)/shard_map/psum | solution.py:79
  76.8 25.6 %copy-start.4 = (f32[16,8]{0,1:T(8,128)S(1)}, f32[16,8]{0,1:T(8,128)}, u32[]{:S(2)}) copy-start(f32[16,8]{0,1:T(8,128)} %param.20) | copy-start | bytes 1540
  76.8 41.1 %copy-start.1 = (f32[16,1024]{1,0:T(8,128)S(1)}, f32[16,1024]{1,0:T(8,128)}, u32[]{:S(2)}) copy-start(f32[16,1024]{1,0:T(8,128)} %all-reduce.3.cloned.1.call-done) | copy-start | bytes 196612
  95.4 22.4 %all-to-all-start.1 = ((f32[16,8,1024]{2,1,0:T(8,128)}), f32[16,8,1024]{2,1,0:T(8,128)}, u32[]{:S(2)}, u32[]{:S(2)}) async-start(f32[16,8,1024]{2,1,0:T(8,128)} %bitcast.50), calls=%async_computation.1 | async-start | bytes 1048576 | tf_op jit(solution)/shard_map/all_to_all | solution.py:82
Sparse Core Ops, SparseCore 0:
  26.3 17.9 all-reduce.2
  76.9 16.4 all-reduce.4
where the time goes:
time: 128 us; the launch traced here: 127 us
  waiting for transfers between devices  49.9 us (39%)
  blocking collectives  33.1 us (26%)
  matrix products  18.6 us (15%)
  between operations  13.5 us (11%)
  starting transfers between devices  6.92 us (5%)
  other arithmetic  3 us (2%)
  local copies, waits for them, and re-layouts  2.23 us (2%)
    psum x1, waiting for transfers between devices, local(): projected = lax.psum(projected, 'head')  17.7 us
    psum x1, waiting for transfers between devices, local(): expert_out = lax.psum(expert_out, 'head')  16.7 us
    all_to_all x1, waiting for transfers between devices, local(): lax.all_to_all(pieces, ('req', 'exp'), split_axis=0, concat_axis=0, tiled...  15.4 us
    all_to_all x1, blocking collectives, local(): lax.all_to_all(outgoing, ('req', 'exp'), split_axis=0, concat_axis=0, til...  13 us
    psum x1, blocking collectives, local(): squares = lax.psum(jnp.sum(hidden * hidden, axis=1), 'exp')  10.1 us
    all_gather x1, blocking collectives, local(): lax.all_gather(attended, 'exp', axis=0, tiled=True)  9.94 us
    all_to_all x1, starting transfers between devices, local(): lax.all_to_all(pieces, ('req', 'exp'), split_axis=0, concat_axis=0, tiled...  6.88 us
    dot_general x1, matrix products, local(): jnp.dot(lax.all_gather(attended, 'exp', axis=0, tiled=True), out_weight,...  5.21 us
  transfers between devices with their start and end apart: 3, of which 3 were waited for; matrix products, arithmetic and copies ran while one was open for 0% of the time, Pallas kernels for 0%

commit v1 on v0

v1 whole, which is shorter than its diff:
```python
import functools
import math

import jax
import jax.numpy as jnp
from jax import lax
from jax.experimental import pallas as pl
from jax.experimental.pallas import tpu as pltpu
from jax.sharding import PartitionSpec as P

F32 = jnp.float32
BF16 = jnp.bfloat16


def whole(memory_space=pltpu.VMEM):
    return pl.BlockSpec(memory_space=memory_space)


def attend_kernel(len_ref, q_ref, k_hbm, v_hbm, o_ref, kbuf, vbuf, scr, sems, *, kv_heads):
    rows, heads, size = q_ref.shape
    per = heads // kv_heads

    def copies(t):
        return (
            pltpu.make_async_copy(k_hbm.at[t], kbuf.at[t], sems.at[0, t]),
            pltpu.make_async_copy(v_hbm.at[t], vbuf.at[t], sems.at[1, t]),
        )

    for t in range(rows):
        for c in copies(t):
            c.start()
    width = kbuf.shape[1]
    col = lax.broadcasted_iota(jnp.int32, (heads, width), 1)
    row = lax.broadcasted_iota(jnp.int32, (heads, width), 0)
    same = (col % kv_heads) == (row // per)
    slot = jnp.where(same, col // kv_heads, jnp.int32(2**30))
    for t in range(rows):
        kc, vc = copies(t)
        kc.wait()
        logits = lax.dot_general(
            q_ref[t], kbuf[t], (((1,), (1,)), ((), ())), preferred_element_type=F32
        ) * (1.0 / math.sqrt(size))
        logits = jnp.where(slot < len_ref[t], logits, -1e30)
        raised = jnp.exp(logits - jnp.max(logits, axis=1, keepdims=True))
        weights = (raised / jnp.sum(raised, axis=1, keepdims=True)).astype(BF16)
        vc.wait()
        scr[t * heads : (t + 1) * heads, :] = jnp.dot(weights, vbuf[t], preferred_element_type=F32)
    for j in range(heads):
        o_ref[:, j * size : (j + 1) * size] = scr[pl.ds(j, rows, stride=heads), :].astype(BF16)


def attend(queries, keys, values, lengths):
    rows, heads, size = queries.shape
    slots, kv_heads = keys.shape[1:3]
    flat = (rows, slots * kv_heads, size)
    return pl.pallas_call(
        functools.partial(attend_kernel, kv_heads=kv_heads),
        out_shape=jax.ShapeDtypeStruct((rows, heads * size), BF16),
        in_specs=[whole(pltpu.SMEM), whole(), whole(pl.ANY), whole(pl.ANY)],
        out_specs=whole(),
        scratch_shapes=[
            pltpu.VMEM(flat, BF16),
            pltpu.VMEM(flat, BF16),
            pltpu.VMEM((rows * heads, size), F32),
            pltpu.SemaphoreType.DMA((2, rows)),
        ],
        name="attend",
    )(lengths, queries, keys.reshape(flat), values.reshape(flat))


def project_kernel(src_ref, *refs, pieces, chunks):
    parts = refs[:pieces]
    w_hbm, o_ref, xs, wbuf, sems = refs[pieces:]
    depth = w_hbm.shape[0]
    step = depth // chunks

    def copy(c):
        sl = pl.ds(c * step, step)
        return pltpu.make_async_copy(w_hbm.at[sl], wbuf.at[sl], sems.at[c])

    for c in range(chunks):
        copy(c).start()
    loaded = [p[...].astype(F32) for p in parts]
    if pieces > 1:
        blocks = []
        for b in range(pieces):
            picked = loaded[0]
            for k in range(1, pieces):
                picked = jnp.where(src_ref[k] == b, loaded[k], picked)
            blocks.append(picked)
        x = jnp.concatenate(blocks, axis=0)
    else:
        x = loaded[0]
    xs[...] = x.astype(BF16)
    acc = None
    for c in range(chunks):
        copy(c).wait()
        sl = slice(c * step, (c + 1) * step)
        part = jnp.dot(xs[:, sl], wbuf[sl, :], preferred_element_type=F32)
        acc = part if acc is None else acc + part
    o_ref[...] = acc


def project(source, parts, out_weight, rows):
    depth, width = out_weight.shape
    chunks = 8
    return pl.pallas_call(
        functools.partial(project_kernel, pieces=len(parts), chunks=chunks),
        out_shape=jax.ShapeDtypeStruct((rows, width), F32),
        in_specs=[whole(pltpu.SMEM)] + [whole()] * len(parts) + [whole(pl.ANY)],
        out_specs=whole(),
        scratch_shapes=[
            pltpu.VMEM((rows, depth), BF16),
            pltpu.VMEM((depth, width), BF16),
            pltpu.SemaphoreType.DMA((chunks,)),
        ],
        name="project",
    )(source, *parts, out_weight)


def dispatch_kernel(own_ref, other_ref, resid_ref, sel_ref, hid_ref, out_ref):
    hidden = resid_ref[...].astype(F32) + (own_ref[...] + other_ref[...])
    hid_ref[...] = hidden
    out_ref[...] = jnp.dot(sel_ref[...], hidden.astype(BF16), preferred_element_type=F32).astype(BF16)


def dispatch(own, other, resid, selector):
    rows, width = resid.shape
    return pl.pallas_call(
        dispatch_kernel,
        out_shape=(
            jax.ShapeDtypeStruct((rows, width), F32),
            jax.ShapeDtypeStruct((selector.shape[0], width), BF16),
        ),
        in_specs=[whole()] * 4,
        out_specs=(whole(), whole()),
        name="dispatch",
    )(own, other, resid, selector)


def expert_kernel(x_ref, gain_ref, wg_hbm, wu_hbm, wd_hbm, o_ref, wbuf, dbuf, sems, dsems, *, groups, cols):
    items, width = x_ref.shape[1:]
    depth = cols * width
    hid = wg_hbm.shape[1]
    step = 512
    chunks = depth // step

    def copies(c):
        sl = pl.ds(c * step, step)
        return (
            pltpu.make_async_copy(wg_hbm.at[sl], wbuf.at[sl, pl.ds(0, hid)], sems.at[0, c]),
            pltpu.make_async_copy(wu_hbm.at[sl], wbuf.at[sl, pl.ds(hid, hid)], sems.at[1, c]),
        )

    down = pltpu.make_async_copy(wd_hbm, dbuf, dsems.at[0])
    for c in range(chunks):
        for d in copies(c):
            d.start()
    down.start()

    def column(e):
        return jnp.concatenate([x_ref[s * cols + e].astype(F32) for s in range(groups)], axis=0)

    squares = None
    for e in range(cols):
        x = column(e)
        part = jnp.sum(x * x, axis=1, keepdims=True)
        squares = part if squares is None else squares + part
    inverse = lax.rsqrt(squares / depth + 1e-06)
    normed = jnp.concatenate(
        [
            (column(e) * inverse * gain_ref[:, e * width : (e + 1) * width]).astype(BF16)
            for e in range(cols)
        ],
        axis=1,
    )
    acc = None
    for c in range(chunks):
        for d in copies(c):
            d.wait()
        sl = slice(c * step, (c + 1) * step)
        part = jnp.dot(normed[:, sl], wbuf[sl, :], preferred_element_type=F32)
        acc = part if acc is None else acc + part
    gate, up = acc[:, :hid], acc[:, hid:]
    activated = (gate / (1.0 + jnp.exp(-gate)) * up).astype(BF16)
    down.wait()
    for e in range(cols):
        y = jnp.dot(
            activated, dbuf[:, e * width : (e + 1) * width], preferred_element_type=F32
        ).astype(BF16)
        for s in range(groups):
            o_ref[s * cols + e] = y[s * items : (s + 1) * items, :]


def expert(arrived, gain, w_gate, w_up, w_down, groups, cols):
    depth, hid = w_gate.shape
    chunks = depth // 512
    return pl.pallas_call(
        functools.partial(expert_kernel, groups=groups, cols=cols),
        out_shape=jax.ShapeDtypeStruct(arrived.shape, BF16),
        in_specs=[whole(), whole(), whole(pl.ANY), whole(pl.ANY), whole(pl.ANY)],
        out_specs=whole(),
        scratch_shapes=[
            pltpu.VMEM((depth, 2 * hid), BF16),
            pltpu.VMEM((hid, depth), BF16),
            pltpu.SemaphoreType.DMA((2, chunks)),
            pltpu.SemaphoreType.DMA((1,)),
        ],
        name="expert",
    )(arrived, gain, w_gate, w_up, w_down)


def combine_kernel(spread_ref, y_ref, o_ref):
    rows = spread_ref.shape[0]
    spread = spread_ref[...]
    high = spread.astype(BF16)
    rest = spread - high.astype(F32)
    mid = rest.astype(BF16)
    low = (rest - mid.astype(F32)).astype(BF16)
    stacked = jnp.concatenate([high, mid, low], axis=0)
    res = jnp.dot(stacked, y_ref[...], preferred_element_type=F32)
    o_ref[...] = res[:rows] + (res[rows : 2 * rows] + res[2 * rows :])


def combine(spread, returned):
    return pl.pallas_call(
        combine_kernel,
        out_shape=jax.ShapeDtypeStruct((spread.shape[0], returned.shape[1]), F32),
        in_specs=[whole(), whole()],
        out_specs=whole(),
        name="combine",
    )(spread, returned)


def local(
    queries,
    keys,
    values,
    lengths,
    out_weight,
    resid,
    norm_gain,
    expert_ids,
    route_weights,
    w_gate,
    w_up,
    w_down,
):
    req_count = lax.axis_size("req")
    exp_count = lax.axis_size("exp")
    column = lax.axis_index("exp")
    rows_dev = queries.shape[0]
    group_rows, col_width = resid.shape
    capacity = 2 * rows_dev
    expert_total = req_count * exp_count

    def swap(x):
        return lax.ppermute(x, "head", [(0, 1), (1, 0)])

    attended = attend(queries, keys, values, lengths)
    if exp_count == 4:
        source = column ^ jnp.arange(exp_count, dtype=jnp.int32)
        parts = [attended] + [
            lax.ppermute(attended, "exp", [(i, i ^ k) for i in range(exp_count)])
            for k in range(1, exp_count)
        ]
    else:
        source = jnp.zeros((1,), jnp.int32)
        parts = [lax.all_gather(attended, "exp", axis=0, tiled=True)]

    matched = expert_ids[:, :, None] == jnp.arange(expert_total, dtype=jnp.int32)[None, None, :]
    chosen = jnp.any(matched, axis=1)
    weighting = jnp.sum(jnp.where(matched, route_weights[:, :, None], 0.0), axis=1)
    position = jnp.cumsum(chosen.astype(jnp.int32), axis=0) - 1
    selector = (
        position.T[:, None, :] == jnp.arange(capacity, dtype=jnp.int32)[None, :, None]
    ) & chosen.T[:, None, :]
    spread = jnp.where(selector, weighting.T[:, None, :], 0.0)
    spread = spread.reshape(expert_total * capacity, group_rows).T
    selector = selector.astype(BF16).reshape(expert_total * capacity, group_rows)

    own = project(source, parts, out_weight, group_rows)
    hidden, outgoing = dispatch(own, swap(own), resid, selector)
    outgoing = outgoing.reshape(expert_total, capacity, col_width)
    arrived = lax.all_to_all(outgoing, ("req", "exp"), split_axis=0, concat_axis=0, tiled=True)
    made = expert(
        arrived, norm_gain[None, :], w_gate[0], w_up[0], w_down[0], req_count, exp_count
    )
    returned = lax.all_to_all(made, ("req", "exp"), split_axis=0, concat_axis=0, tiled=True)
    mixture = combine(spread, returned.reshape(expert_total * capacity, col_width))
    return (hidden + (mixture + swap(mixture))).astype(BF16)


def solution(mesh):
    in_specs = (
        P(("req", "exp"), "head", None),
        P(("req", "exp"), None, "head", None),
        P(("req", "exp"), None, "head", None),
        P(("req", "exp")),
        P("head", "exp"),
        P("req", "exp"),
        P(),
        P("req", None),
        P("req", None),
        P(("req", "exp"), None, "head"),
        P(("req", "exp"), None, "head"),
        P(("req", "exp"), "head", None),
    )
    out_specs = P("req", "exp")
    return jax.shard_map(local, mesh=mesh, in_specs=in_specs, out_specs=out_specs, check_vma=False)
```

time: 128 us -> 65.3 us (0.51)
  waiting for transfers between devices: 49.9 us -> 2.64 us
  Pallas kernels: 0 us -> 19.8 us
  matrix products: 18.6 us -> 0 us
  between operations: 13.5 us -> 0.09 us
  blocking collectives: 33.1 us -> 30.4 us
  starting transfers between devices: 6.92 us -> 4.71 us
  local copies, waits for them, and re-layouts: 2.23 us -> 4.11 us
    psum x2 -> x0, waiting for transfers between devices: 34.4 us -> none  [the longest x1 17.7 us: local(): projected = lax.psum(projected, 'head')]
    pallas_call x0 -> x5, Pallas kernels: none -> 19.8 us  [the longest x1 6.43 us: expert(): pl.pallas_call(functools.partial(expert_kernel, groups=groups, cols=cols)...]
    dot_general x7 -> x0, matrix products: 18.6 us -> none  [the longest x1 5.21 us: local(): jnp.dot(lax.all_gather(attended, 'exp', axis=0, tiled=True), out_weight,...]
    all_to_all x1 -> x0, waiting for transfers between devices: 15.4 us -> none  [local(): lax.all_to_all(pieces, ('req', 'exp'), split_axis=0, concat_axis=0, tiled...]
    all_to_all x0 -> x1, blocking collectives: none -> 13.2 us  [local(): lax.all_to_all(made, ('req', 'exp'), split_axis=0, concat_axis=0, tiled=T...]
    psum x1 -> x0, blocking collectives: 10.1 us -> none  [local(): squares = lax.psum(jnp.sum(hidden * hidden, axis=1), 'exp')]
    all_gather x1 -> x0, blocking collectives: 9.94 us -> none  [local(): lax.all_gather(attended, 'exp', axis=0, tiled=True)]
    all_to_all x1 -> x0, starting transfers between devices: 6.88 us -> none  [local(): lax.all_to_all(pieces, ('req', 'exp'), split_axis=0, concat_axis=0, tiled...]
  transfers between devices with their start and end apart: 3 -> 5, of which waited for: 3 -> 4; matrix products, arithmetic and copies ran while one was open for 0% -> 7% of each run, Pallas kernels for 0% -> 0%
where the time goes in v1:
time: 65.3 us; the launch traced here: 64.6 us
  blocking collectives  30.4 us (47%)
  Pallas kernels  19.8 us (30%)
  starting transfers between devices  4.71 us (7%)
  local copies, waits for them, and re-layouts  4.11 us (6%)
  other arithmetic  2.89 us (4%)
  waiting for transfers between devices  2.64 us (4%)
    all_to_all x1, blocking collectives, local(): lax.all_to_all(outgoing, ('req', 'exp'), split_axis=0, concat_axis=0, til...  17.3 us
    all_to_all x1, blocking collectives, local(): lax.all_to_all(made, ('req', 'exp'), split_axis=0, concat_axis=0, tiled=T...  13.2 us
    pallas_call x1, Pallas kernels, expert(): pl.pallas_call(functools.partial(expert_kernel, groups=groups, cols=cols)...  6.43 us
    pallas_call x1, Pallas kernels, project(): pl.pallas_call(functools.partial(project_kernel, pieces=len(parts), chunk...  5.17 us
    ppermute x3, starting transfers between devices, local(): lax.ppermute(attended, 'exp', [(i, i ^ k) for i in range(exp_count)])  4.63 us
    pallas_call x1, Pallas kernels, attend(): pl.pallas_call(functools.partial(attend_kernel, kv_heads=kv_heads), out_s...  4.62 us
    unnamed x12, local copies, waits for them, and re-layouts  2.84 us
    pallas_call x1, Pallas kernels, dispatch(): pl.pallas_call(dispatch_kernel, out_shape=(jax.ShapeDtypeStruct((rows, wi...  1.77 us
  transfers between devices with their start and end apart: 5, of which 4 were waited for; matrix products, arithmetic and copies ran while one was open for 7% of the time, Pallas kernels for 0%

profile of v1, /device:TPU:0, one launch (start us, length us, event | category | flops | bytes accessed | tf_op | source)
XLA Modules:
  0.0 64.6 jit_solution(17250788467941280966)
XLA Ops:
  0.0 4.6 %attend.1.refs_0_ = bf16[4,4096]{1,0:T(4,128)(2,1)} custom-call(s32[4]{0:T(128)} %len_ref.1, bf16[4,32,128]{2,1,0:T(8,128)(2,1)} %q_ref.1, bf16[4,1024,128]{2,1,0:T(8,128)(2,1)} %bitcast.23, bf16[4,1024,128]{2,1,0:T(8,128)(2,1)} %bitcast.24), custom_call_target="tpu_custom_call" | custom-call | tf_op jit(solution)/shard_map/attend/pallas_call | solution.py:56
  4.6 4.0 %collective-permute-start.2 = (bf16[4,4096]{1,0:T(4,128)(2,1)}, bf16[4,4096]{1,0:T(4,128)(2,1)S(1)}, u32[]{:S(2)}, u32[]{:S(2)}) collective-permute-start(bf16[4,4096]{1,0:T(4,128)(2,1)} %attend.1.refs_0_), channel_id=1, source_target_pairs={{0,3},{1,2},{2,1},{3,0},{4,7},{5,6},{6,5},{7,4},{8,11},{9,10},{10,... | collective-permute-start | bytes 98312 | tf_op jit(solution)/shard_map/ppermute | solution.py:264
  8.6 0.5 collective-permute-start.1
  9.1 0.1 collective-permute-start
  9.3 0.8 %copy.24 = s32[16,8]{1,0:T(8,128)S(1)} copy(s32[16,8]{0,1:T(8,128)} %param.19) | data formatting | bytes 1024 | tf_op args[7]
  10.0 0.1 fusion
  10.1 0.1 copy.27
  10.3 0.1 copy.25
  10.3 0.8 %copy.30 = f32[16,8]{1,0:T(8,128)S(1)} copy(f32[16,8]{0,1:T(8,128)} %param.20) | data formatting | bytes 1024 | tf_op args[8]
  11.1 0.1 select_reduce_fusion
  11.2 0.1 copy.31
  11.3 0.6 iota_xor_fusion.src_ref
  11.9 0.1 eq.40
  12.1 0.1 copy.32
  12.1 0.1 copy.26
  12.2 0.5 collective-permute-done.1.refs_2_
  12.7 0.5 collective-permute-done.refs_1_
  13.3 0.1 copy-done.3
  13.4 0.6 copy-done.4
  14.0 5.2 %project.1.own_ref = f32[16,1024]{1,0:T(8,128)} custom-call(s32[4]{0:T(128)} %iota_xor_fusion.src_ref, bf16[4,4096]{1,0:T(4,128)(2,1)} %attend.1.refs_0_, bf16[4,4096]{1,0:T(4,128)(2,1)} %copy-done.4, bf16[4,4096]{1,0:T(4,128)(2,1)} %copy-done.3, bf16[4,4096]{1,0:T(4,128)(2,1)} %copy-done.2, bf16[4096,1024]{1,0:T(8,128)(2,1)} %refs_4_.1), custom_call_target="tpu_custom_call" | custom-call | tf_op jit(solution)/shard_map/project/pallas_call | solution.py:107
  19.1 0.1 collective-permute-start.3
  19.2 0.6 select_bitcast_fusion
  19.8 0.7 %copy.29.sel_ref = bf16[128,16]{1,0:T(8,128)(2,1)} copy(bf16[128,16]{0,1:T(8,128)(2,1)S(1)} %convert_element_type.11) | data formatting | bytes 8192 | tf_op jit(solution)/shard_map/convert_element_type | solution.py:280
  20.5 0.1 collective-permute-done.3.other_ref
  20.7 0.6 copy-done.1
  21.3 1.8 %dispatch.1 = (f32[16,1024]{1,0:T(8,128)}, bf16[128,1024]{1,0:T(8,128)(2,1)}) custom-call(f32[16,1024]{1,0:T(8,128)} %project.1.own_ref, f32[16,1024]{1,0:T(8,128)} %copy-done.1, bf16[16,1024]{1,0:T(8,128)(2,1)} %resid_ref.1, bf16[128,16]{1,0:T(8,128)(2,1)} %copy.29.sel_ref), custom_call_target="tpu_custom_call" | custom-call | tf_op jit(solution)/shard_map/dispatch/pallas_call | solution.py:129
  23.1 17.3 %all_to_all.10.x_ref = bf16[16,8,1024]{2,1,0:T(8,128)(2,1)} all-to-all(bf16[16,8,1024]{2,1,0:T(8,128)(2,1)} %bitcast.26), channel_id=1, replica_groups=mesh['req'=4,'head'=2,'exp'=4] {'req','exp'}, dimensions={0} | all-to-all | bytes 524288 | tf_op jit(solution)/shard_map/all_to_all | solution.py:285
  40.3 6.4 %expert.1 = bf16[16,8,1024]{2,1,0:T(8,128)(2,1)} custom-call(bf16[16,8,1024]{2,1,0:T(8,128)(2,1)} %all_to_all.10.x_ref, f32[1,4096]{1,0:T(1,128)} %bitcast.29, bf16[4096,384]{1,0:T(8,128)(2,1)} %bitcast.20, bf16[4096,384]{1,0:T(8,128)(2,1)} %bitcast.21, bf16[384,4096]{1,0:T(8,128)(2,1)} %bitcast.22), custom_call_target="tpu_custom_call" | custom-call | tf_op jit(solution)/shard_map/expert/pallas_call | solution.py:198
  46.8 13.2 %all_to_all.11 = bf16[16,8,1024]{2,1,0:T(8,128)(2,1)} all-to-all(bf16[16,8,1024]{2,1,0:T(8,128)(2,1)} %expert.1), channel_id=1, replica_groups=mesh['req'=4,'head'=2,'exp'=4] {'req','exp'}, dimensions={0} | all-to-all | bytes 524288 | tf_op jit(solution)/shard_map/all_to_all | solution.py:289
  59.9 1.8 %combine.1 = f32[16,1024]{1,0:T(8,128)} custom-call(f32[16,128]{1,0:T(8,128)} %get-tuple-element.9.spread_ref, bf16[128,1024]{1,0:T(8,128)(2,1)} %bitcast.25), custom_call_target="tpu_custom_call" | custom-call | tf_op jit(solution)/shard_map/combine/pallas_call | solution.py:226
  61.7 1.5 %collective-permute-done.4 = f32[16,1024]{1,0:T(8,128)S(1)} collective-permute-done((f32[16,1024]{1,0:T(8,128)}, f32[16,1024]{1,0:T(8,128)S(1)}, u32[]{:S(2)}, u32[]{:S(2)}) %collective-permute-start.4) | collective-permute-done | bytes 65568 | tf_op jit(solution)/shard_map/ppermute | solution.py:258
  63.1 1.5 %add_convert_fusion = bf16[16,1024]{1,0:T(8,128)(2,1)} fusion(f32[16,1024]{1,0:T(8,128)S(1)} %copy-done, f32[16,1024]{1,0:T(8,128)} %combine.1, f32[16,1024]{1,0:T(8,128)S(1)} %collective-permute-done.4), kind=kLoop, calls=%fused_computation | loop fusion | flops 49152 | bytes 229376 | tf_op jit(solution)/shard_map/convert_element_type | solution.py:291
  (18 shorter events, 0.2 us)
Async XLA Ops:
  4.6 7.6 %collective-permute-start.2 = (bf16[4,4096]{1,0:T(4,128)(2,1)}, bf16[4,4096]{1,0:T(4,128)(2,1)S(1)}, u32[]{:S(2)}, u32[]{:S(2)}) collective-permute-start(bf16[4,4096]{1,0:T(4,128)(2,1)} %attend.1.refs_0_), channel_id=1, source_target_pairs={{0,3},{1,2},{2,1},{3,0},{4,7},{5,6},{6,5},{7,4},{8,11},{9,10},{10,... | collective-permute-start | bytes 98312 | tf_op jit(solution)/shard_map/ppermute | solution.py:264
  8.6 4.1 %collective-permute-start.1 = (bf16[4,4096]{1,0:T(4,128)(2,1)}, bf16[4,4096]{1,0:T(4,128)(2,1)S(1)}, u32[]{:S(2)}, u32[]{:S(2)}) collective-permute-start(bf16[4,4096]{1,0:T(4,128)(2,1)} %attend.1.refs_0_), channel_id=1, source_target_pairs={{0,2},{1,3},{2,0},{3,1},{4,6},{5,7},{6,4},{7,5},{8,10},{9,11},{10,... | collective-permute-start | bytes 98312 | tf_op jit(solution)/shard_map/ppermute | solution.py:264
  9.1 4.1 %collective-permute-start = (bf16[4,4096]{1,0:T(4,128)(2,1)}, bf16[4,4096]{1,0:T(4,128)(2,1)S(1)}, u32[]{:S(2)}, u32[]{:S(2)}) collective-permute-start(bf16[4,4096]{1,0:T(4,128)(2,1)} %attend.1.refs_0_), channel_id=1, source_target_pairs={{0,1},{1,0},{2,3},{3,2},{4,5},{5,4},{6,7},{7,6},{8,9},{9,8},{10,11... | collective-permute-start | bytes 98312 | tf_op jit(solution)/shard_map/ppermute | solution.py:264
  12.2 1.1 %copy-start.2 = (bf16[4,4096]{1,0:T(4,128)(2,1)}, bf16[4,4096]{1,0:T(4,128)(2,1)S(1)}, u32[]{:S(2)}) copy-start(bf16[4,4096]{1,0:T(4,128)(2,1)S(1)} %collective-permute-done.2.refs_3_) | copy-start | bytes 98308
  12.7 0.6 copy-start.3
  13.4 0.6 copy-start.4
  19.1 1.5 %collective-permute-start.3 = (f32[16,1024]{1,0:T(8,128)}, f32[16,1024]{1,0:T(8,128)S(1)}, u32[]{:S(2)}, u32[]{:S(2)}) collective-permute-start(f32[16,1024]{1,0:T(8,128)} %project.1.own_ref), channel_id=1, source_target_pairs={{0,4},{4,0},{1,5},{5,1},{2,6},{6,2},{3,7},{7,3},{8,12},{12,8},{9,1... | collective-permute-start | bytes 196616 | tf_op jit(solution)/shard_map/ppermute | solution.py:258
  20.7 0.6 copy-start.1
  40.3 22.8 %copy-start = (f32[16,1024]{1,0:T(8,128)S(1)}, f32[16,1024]{1,0:T(8,128)}, u32[]{:S(2)}) copy-start(f32[16,1024]{1,0:T(8,128)} %get-tuple-element.7) | copy-start | bytes 196612
  61.7 1.5 %collective-permute-start.4 = (f32[16,1024]{1,0:T(8,128)}, f32[16,1024]{1,0:T(8,128)S(1)}, u32[]{:S(2)}, u32[]{:S(2)}) collective-permute-start(f32[16,1024]{1,0:T(8,128)} %combine.1), channel_id=1, source_target_pairs={{0,4},{4,0},{1,5},{5,1},{2,6},{6,2},{3,7},{7,3},{8,12},{12,8},{9,1... | collective-permute-start | bytes 196616 | tf_op jit(solution)/shard_map/ppermute | solution.py:258

commit v2 on v1

v2 whole, which is shorter than its diff:
```python
import functools
import math

import jax
import jax.numpy as jnp
from jax import lax
from jax.experimental import pallas as pl
from jax.experimental.pallas import tpu as pltpu
from jax.sharding import PartitionSpec as P

F32 = jnp.float32
BF16 = jnp.bfloat16


def whole(memory_space=pltpu.VMEM):
    return pl.BlockSpec(memory_space=memory_space)


def near(x):
    return pltpu.with_memory_space_constraint(x, pltpu.VMEM)


def far(x):
    return pltpu.with_memory_space_constraint(x, pltpu.HBM)


def attend_kernel(
    len_hbm, q_hbm, k_hbm, v_hbm, w_hbm, o_ref, w_ref, len_ref, q_ref, kbuf, vbuf, scr, sems, one,
    *, kv_heads
):
    rows, heads, size = q_ref.shape
    per = heads // kv_heads

    def copies(t):
        return (
            pltpu.make_async_copy(k_hbm.at[t], kbuf.at[t], sems.at[0, t]),
            pltpu.make_async_copy(v_hbm.at[t], vbuf.at[t], sems.at[1, t]),
        )

    ask = pltpu.make_async_copy(q_hbm, q_ref, one.at[0])
    load = pltpu.make_async_copy(w_hbm, w_ref, one.at[1])
    span = pltpu.make_async_copy(len_hbm, len_ref, one.at[2])
    ask.start()
    span.start()
    for t in range(rows):
        for c in copies(t):
            c.start()
    load.start()
    width = kbuf.shape[1]
    col = lax.broadcasted_iota(jnp.int32, (heads, width), 1)
    row = lax.broadcasted_iota(jnp.int32, (heads, width), 0)
    same = (col % kv_heads) == (row // per)
    slot = jnp.where(same, col // kv_heads, jnp.int32(2**30))
    ask.wait()
    span.wait()
    for t in range(rows):
        kc, vc = copies(t)
        kc.wait()
        logits = lax.dot_general(
            q_ref[t], kbuf[t], (((1,), (1,)), ((), ())), preferred_element_type=F32
        ) * (1.0 / math.sqrt(size))
        logits = jnp.where(slot < len_ref[t], logits, -1e30)
        raised = jnp.exp(logits - jnp.max(logits, axis=1, keepdims=True))
        weights = (raised / jnp.sum(raised, axis=1, keepdims=True)).astype(BF16)
        vc.wait()
        scr[t * heads : (t + 1) * heads, :] = jnp.dot(weights, vbuf[t], preferred_element_type=F32)
    for j in range(heads):
        o_ref[:, j * size : (j + 1) * size] = scr[pl.ds(j, rows, stride=heads), :].astype(BF16)
    load.wait()


def attend(queries, keys, values, lengths, out_weight):
    rows, heads, size = queries.shape
    slots, kv_heads = keys.shape[1:3]
    flat = (rows, slots * kv_heads, size)
    return pl.pallas_call(
        functools.partial(attend_kernel, kv_heads=kv_heads),
        out_shape=(
            pltpu.VMEM((rows, heads * size), BF16),
            pltpu.VMEM(out_weight.shape, BF16),
        ),
        in_specs=[whole(pltpu.HBM)] * 5,
        out_specs=(whole(), whole()),
        scratch_shapes=[
            pltpu.SMEM((rows,), jnp.int32),
            pltpu.VMEM(queries.shape, BF16),
            pltpu.VMEM(flat, BF16),
            pltpu.VMEM(flat, BF16),
            pltpu.VMEM((rows * heads, size), F32),
            pltpu.SemaphoreType.DMA((2, rows)),
            pltpu.SemaphoreType.DMA((3,)),
        ],
        compiler_params=pltpu.CompilerParams(vmem_limit_bytes=16 * 2**20),
        name="attend",
    )(*map(far, (lengths, queries, keys.reshape(flat), values.reshape(flat), out_weight)))


def route_kernel(ids_ref, weight_ref, sel_ref, spread_ref, *, capacity):
    total, rows = sel_ref.shape
    experts = total // capacity
    expert = lax.broadcasted_iota(jnp.int32, (experts, rows), 0)
    chosen = jnp.zeros((experts, rows), F32)
    weight = jnp.zeros((experts, rows), F32)
    for k in range(ids_ref.shape[0]):
        hit = ids_ref[k : k + 1, :] == expert
        chosen = jnp.where(hit, 1.0, chosen)
        weight = weight + jnp.where(hit, weight_ref[k : k + 1, :], 0.0)
    before = lax.broadcasted_iota(jnp.int32, (rows, rows), 0)
    after = lax.broadcasted_iota(jnp.int32, (rows, rows), 1)
    upto = jnp.where(before <= after, 1.0, 0.0).astype(BF16)
    place = jnp.dot(chosen.astype(BF16), upto, preferred_element_type=F32) - 1.0
    place = jnp.where(chosen > 0.0, place, -1.0)
    seat = lax.broadcasted_iota(jnp.int32, (experts, capacity, rows), 1).astype(F32)
    taken = jnp.broadcast_to(place[:, None, :], seat.shape) == seat
    shares = jnp.where(taken, jnp.broadcast_to(weight[:, None, :], seat.shape), 0.0)
    sel_ref[...] = jnp.where(taken, 1.0, 0.0).reshape(total, rows).astype(BF16)
    spread_ref[...] = shares.reshape(total, rows).T


def route(expert_ids, route_weights, experts, capacity):
    rows = expert_ids.shape[0]
    total = experts * capacity
    return pl.pallas_call(
        functools.partial(route_kernel, capacity=capacity),
        out_shape=(pltpu.VMEM((total, rows), BF16), pltpu.VMEM((rows, total), F32)),
        in_specs=[whole(), whole()],
        out_specs=(whole(), whole()),
        compiler_params=pltpu.CompilerParams(vmem_limit_bytes=8 * 2**20),
        name="route",
    )(expert_ids.T, route_weights.T)


def project_kernel(*refs, pieces):
    parts = refs[:pieces]
    w_ref, wg_hbm, wu_hbm, wd_hbm, o_ref, both_ref, down_ref, sems = refs[pieces:]
    hid = wg_hbm.shape[1]
    loads = (
        pltpu.make_async_copy(wg_hbm, both_ref.at[:, pl.ds(0, hid)], sems.at[0]),
        pltpu.make_async_copy(wu_hbm, both_ref.at[:, pl.ds(hid, hid)], sems.at[1]),
        pltpu.make_async_copy(wd_hbm, down_ref, sems.at[2]),
    )
    for c in loads:
        c.start()
    loaded = [p[...].astype(F32) for p in parts]
    if pieces > 1:
        place = lax.axis_index("exp")
        blocks = []
        for b in range(pieces):
            picked = loaded[0]
            for k in range(1, pieces):
                picked = jnp.where((place ^ k) == b, loaded[k], picked)
            blocks.append(picked)
        x = jnp.concatenate(blocks, axis=0)
    else:
        x = loaded[0]
    o_ref[...] = jnp.dot(x.astype(BF16), w_ref[...], preferred_element_type=F32)
    for c in loads:
        c.wait()


def project(parts, out_weight, w_gate, w_up, w_down, rows):
    depth, hid = w_gate.shape
    return pl.pallas_call(
        functools.partial(project_kernel, pieces=len(parts)),
        out_shape=(
            pltpu.VMEM((rows, out_weight.shape[1]), F32),
            pltpu.VMEM((depth, 2 * hid), BF16),
            pltpu.VMEM(w_down.shape, BF16),
        ),
        in_specs=[whole()] * (len(parts) + 1) + [whole(pltpu.HBM)] * 3,
        out_specs=(whole(),) * 3,
        scratch_shapes=[pltpu.SemaphoreType.DMA((3,))],
        compiler_params=pltpu.CompilerParams(vmem_limit_bytes=8 * 2**20),
        name="project",
    )(*map(near, parts), near(out_weight), *map(far, (w_gate, w_up, w_down)))


def dispatch_kernel(own_ref, other_ref, resid_ref, sel_ref, hid_ref, out_ref):
    hidden = resid_ref[...].astype(F32) + (own_ref[...] + other_ref[...])
    hid_ref[...] = hidden
    out_ref[...] = jnp.dot(sel_ref[...], hidden.astype(BF16), preferred_element_type=F32).astype(BF16)


def dispatch(own, other, resid, selector):
    rows, width = resid.shape
    return pl.pallas_call(
        dispatch_kernel,
        out_shape=(
            pltpu.VMEM((rows, width), F32),
            pltpu.VMEM((selector.shape[0], width), BF16),
        ),
        in_specs=[whole()] * 4,
        out_specs=(whole(), whole()),
        compiler_params=pltpu.CompilerParams(vmem_limit_bytes=8 * 2**20),
        name="dispatch",
    )(near(own), near(other), near(resid), near(selector))


def expert_kernel(x_ref, gain_ref, both_ref, wd_ref, o_ref, *, groups, cols):
    items, width = x_ref.shape[1:]
    depth = cols * width
    hid = wd_ref.shape[0]

    def column(e):
        return jnp.concatenate([x_ref[s * cols + e].astype(F32) for s in range(groups)], axis=0)

    squares = None
    for e in range(cols):
        x = column(e)
        part = jnp.sum(x * x, axis=1, keepdims=True)
        squares = part if squares is None else squares + part
    inverse = lax.rsqrt(squares / depth + 1e-06)
    acc = None
    for e in range(cols):
        sl = slice(e * width, (e + 1) * width)
        normed = (column(e) * inverse * gain_ref[:, sl]).astype(BF16)
        part = jnp.dot(normed, both_ref[sl, :], preferred_element_type=F32)
        acc = part if acc is None else acc + part
    gate, up = acc[:, :hid], acc[:, hid:]
    activated = (gate / (1.0 + jnp.exp(-gate)) * up).astype(BF16)
    for e in range(cols):
        y = jnp.dot(
            activated, wd_ref[:, e * width : (e + 1) * width], preferred_element_type=F32
        ).astype(BF16)
        for s in range(groups):
            o_ref[s * cols + e] = y[s * items : (s + 1) * items, :]


def expert(arrived, gain, both, down, groups, cols):
    return pl.pallas_call(
        functools.partial(expert_kernel, groups=groups, cols=cols),
        out_shape=pltpu.VMEM(arrived.shape, BF16),
        in_specs=[whole()] * 4,
        out_specs=whole(),
        compiler_params=pltpu.CompilerParams(vmem_limit_bytes=12 * 2**20),
        name="expert",
    )(*map(near, (arrived, gain, both, down)))


def combine_kernel(spread_ref, y_ref, o_ref):
    rows = spread_ref.shape[0]
    spread = spread_ref[...]
    high = spread.astype(BF16)
    rest = spread - high.astype(F32)
    mid = rest.astype(BF16)
    low = (rest - mid.astype(F32)).astype(BF16)
    stacked = jnp.concatenate([high, mid, low], axis=0)
    res = jnp.dot(stacked, y_ref[...], preferred_element_type=F32)
    o_ref[...] = res[:rows] + (res[rows : 2 * rows] + res[2 * rows :])


def combine(spread, returned):
    return pl.pallas_call(
        combine_kernel,
        out_shape=pltpu.VMEM((spread.shape[0], returned.shape[1]), F32),
        in_specs=[whole(), whole()],
        out_specs=whole(),
        compiler_params=pltpu.CompilerParams(vmem_limit_bytes=8 * 2**20),
        name="combine",
    )(near(spread), near(returned))


def local(
    queries,
    keys,
    values,
    lengths,
    out_weight,
    resid,
    norm_gain,
    expert_ids,
    route_weights,
    w_gate,
    w_up,
    w_down,
):
    req_count = lax.axis_size("req")
    exp_count = lax.axis_size("exp")
    rows_dev = queries.shape[0]
    group_rows, col_width = resid.shape
    capacity = 2 * rows_dev
    expert_total = req_count * exp_count

    def swap(x):
        return lax.ppermute(x, "head", [(0, 1), (1, 0)])

    attended, near_weight = attend(queries, keys, values, lengths, out_weight)
    if exp_count == 4:
        parts = [attended] + [
            lax.ppermute(attended, "exp", [(i, i ^ k) for i in range(exp_count)])
            for k in range(1, exp_count)
        ]
    else:
        parts = [lax.all_gather(attended, "exp", axis=0, tiled=True)]

    selector, spread = route(expert_ids, route_weights, expert_total, capacity)
    parts, selector, spread = lax.optimization_barrier((parts, selector, spread))
    own, both, down = project(parts, near_weight, w_gate[0], w_up[0], w_down[0], group_rows)
    hidden, outgoing = dispatch(own, swap(own), resid, selector)
    outgoing = outgoing.reshape(expert_total, capacity, col_width)
    arrived = lax.all_to_all(outgoing, ("req", "exp"), split_axis=0, concat_axis=0, tiled=True)
    made = expert(arrived, norm_gain[None, :], both, down, req_count, exp_count)
    returned = lax.all_to_all(made, ("req", "exp"), split_axis=0, concat_axis=0, tiled=True)
    mixture = combine(spread, returned.reshape(expert_total * capacity, col_width))
    return (hidden + (mixture + swap(mixture))).astype(BF16)


def solution(mesh):
    in_specs = (
        P(("req", "exp"), "head", None),
        P(("req", "exp"), None, "head", None),
        P(("req", "exp"), None, "head", None),
        P(("req", "exp")),
        P("head", "exp"),
        P("req", "exp"),
        P(),
        P("req", None),
        P("req", None),
        P(("req", "exp"), None, "head"),
        P(("req", "exp"), None, "head"),
        P(("req", "exp"), "head", None),
    )
    out_specs = P("req", "exp")
    return jax.shard_map(local, mesh=mesh, in_specs=in_specs, out_specs=out_specs, check_vma=False)
```

time: 65.3 us -> 51.6 us (0.79)
  Pallas kernels: 19.8 us -> 11.1 us
  local copies, waits for them, and re-layouts: 4.11 us -> 0.01 us
  waiting for transfers between devices: 2.64 us -> 6.11 us
  other arithmetic: 2.89 us -> 0.63 us
  blocking collectives: 30.4 us -> 28.7 us
    pallas_call x1, Pallas kernels: 6.43 us -> 2.21 us  [expert(): pl.pallas_call(functools.partial(expert_kernel, groups=groups, cols=cols)...]
    pallas_call x3 -> x4, Pallas kernels: 8.71 us -> 4.76 us  [the longest x1 4.24 us: project(): pl.pallas_call(functools.partial(project_kernel, pieces=len(parts)), out_...]
    unnamed x12 -> x8, local copies, waits for them, and re-layouts: 2.84 us -> 0.01 us
    ppermute x3, waiting for transfers between devices: 1.05 us -> 3.59 us  [local(): lax.ppermute(attended, 'exp', [(i, i ^ k) for i in range(exp_count)])]
    all_to_all x1, blocking collectives: 17.3 us -> 15.9 us  [local(): lax.all_to_all(outgoing, ('req', 'exp'), split_axis=0, concat_axis=0, til...]
    ppermute x2, waiting for transfers between devices: 1.59 us -> 2.53 us  [swap(): return lax.ppermute(x, 'head', [(0, 1), (1, 0)])]
    convert_element_type x1, other arithmetic: 1.47 us -> 0.63 us  [local(): return (hidden + (mixture + swap(mixture))).astype(BF16)]
    convert_element_type x1 -> x0, local copies, waits for them, and re-layouts: 0.73 us -> none  [local(): selector.astype(BF16).reshape(expert_total * capacity, group_rows)]
  transfers between devices with their start and end apart: 5 -> 5, of which waited for: 4 -> 5; matrix products, arithmetic and copies ran while one was open for 7% -> 0% of each run, Pallas kernels for 0% -> 0%
where the time goes in v2:
time: 51.6 us; the launch traced here: 51.4 us
  blocking collectives  28.7 us (56%)
  Pallas kernels  11.1 us (22%)
  waiting for transfers between devices  6.11 us (12%)
  starting transfers between devices  4.7 us (9%)
  other arithmetic  0.63 us (1%)
    all_to_all x1, blocking collectives, local(): lax.all_to_all(outgoing, ('req', 'exp'), split_axis=0, concat_axis=0, til...  15.9 us
    all_to_all x1, blocking collectives, local(): lax.all_to_all(made, ('req', 'exp'), split_axis=0, concat_axis=0, tiled=T...  12.8 us
    ppermute x3, starting transfers between devices, local(): lax.ppermute(attended, 'exp', [(i, i ^ k) for i in range(exp_count)])  4.63 us
    pallas_call x1, Pallas kernels, project(): pl.pallas_call(functools.partial(project_kernel, pieces=len(parts)), out_...  4.24 us
    pallas_call x1, Pallas kernels, attend(): pl.pallas_call(functools.partial(attend_kernel, kv_heads=kv_heads), out_s...  4.18 us
    ppermute x3, waiting for transfers between devices, local(): lax.ppermute(attended, 'exp', [(i, i ^ k) for i in range(exp_count)])  3.59 us
    ppermute x2, waiting for transfers between devices, swap(): return lax.ppermute(x, 'head', [(0, 1), (1, 0)])  2.53 us
    pallas_call x1, Pallas kernels, expert(): pl.pallas_call(functools.partial(expert_kernel, groups=groups, cols=cols)...  2.21 us
  transfers between devices with their start and end apart: 5, of which 5 were waited for; matrix products, arithmetic and copies ran while one was open for 0% of the time, Pallas kernels for 0%

profile of v2, /device:TPU:0, one launch (start us, length us, event | category | flops | bytes accessed | tf_op | source)
XLA Modules:
  0.0 51.4 jit_solution(15808676586025553855)
XLA Ops:
  0.0 0.0 copy-start.2
  0.0 0.0 copy-start.3
  0.0 4.2 %attend.1 = (bf16[4,4096]{1,0:T(4,128)(2,1)S(1)}, bf16[4096,1024]{1,0:T(8,128)(2,1)S(1)}) custom-call(s32[4]{0:T(128)} %len_hbm.1, bf16[4,32,128]{2,1,0:T(8,128)(2,1)} %q_hbm.1, bf16[4,1024,128]{2,1,0:T(8,128)(2,1)} %bitcast.18, bf16[4,1024,128]{2,1,0:T(8,128)(2,1)} %bitcast.19, bf16[4096,1024]{1,0:T(8,128)(2,1)} %w_hbm.1), custom_call_target="tpu_custom_call" | custom-call | tf_op jit(solution)/shard_map/attend/pallas_call | solution.py:76
  4.2 4.0 %collective-permute-start.2 = (bf16[4,4096]{1,0:T(4,128)(2,1)S(1)}, bf16[4,4096]{1,0:T(4,128)(2,1)S(1)}, u32[]{:S(2)}, u32[]{:S(2)}) collective-permute-start(bf16[4,4096]{1,0:T(4,128)(2,1)S(1)} %get-tuple-element.23.refs_0_), channel_id=1, source_target_pairs={{0,3},{1,2},{2,1},{3,0},{4,7},{5,6},{6,5},{7,4},{8,11},{9,10},{10,... | collective-permute-start | bytes 98312 | tf_op jit(solution)/shard_map/ppermute | solution.py:290
  8.2 0.5 collective-permute-start.1
  8.7 0.1 collective-permute-start
  8.8 0.0 copy-done.2
  8.8 0.0 copy-done.3
  8.8 0.2 route.1
  9.0 1.1 %collective-permute-done.2.refs_3_ = bf16[4,4096]{1,0:T(4,128)(2,1)S(1)} collective-permute-done((bf16[4,4096]{1,0:T(4,128)(2,1)S(1)}, bf16[4,4096]{1,0:T(4,128)(2,1)S(1)}, u32[]{:S(2)}, u32[]{:S(2)}) %collective-permute-start.2) | collective-permute-done | bytes 32800 | tf_op jit(solution)/shard_map/ppermute | solution.py:290
  10.1 2.0 %collective-permute-done.1.refs_2_ = bf16[4,4096]{1,0:T(4,128)(2,1)S(1)} collective-permute-done((bf16[4,4096]{1,0:T(4,128)(2,1)S(1)}, bf16[4,4096]{1,0:T(4,128)(2,1)S(1)}, u32[]{:S(2)}, u32[]{:S(2)}) %collective-permute-start.1) | collective-permute-done | bytes 32800 | tf_op jit(solution)/shard_map/ppermute | solution.py:290
  12.1 0.5 collective-permute-done.refs_1_
  12.6 0.0 copy-start
  12.6 0.0 copy-start.1
  12.6 4.2 %project.1 = (f32[16,1024]{1,0:T(8,128)S(1)}, bf16[4096,768]{1,0:T(8,128)(2,1)S(1)}, bf16[384,4096]{1,0:T(8,128)(2,1)S(1)}) custom-call(bf16[4,4096]{1,0:T(4,128)(2,1)S(1)} %get-tuple-element.23.refs_0_, bf16[4,4096]{1,0:T(4,128)(2,1)S(1)} %collective-permute-done.refs_1_, bf16[4,4096]{1,0:T(4,128)(2,1)S(1)} %collective-permute-done.1.refs_2_, ...), custom_call_target="tpu_custom_call" | custom-call | tf_op jit(solution)/shard_map/project/pallas_call | solution.py:163
  16.9 0.1 collective-permute-start.3
  16.9 1.2 %collective-permute-done.3.other_ref = f32[16,1024]{1,0:T(8,128)S(1)} collective-permute-done((f32[16,1024]{1,0:T(8,128)S(1)}, f32[16,1024]{1,0:T(8,128)S(1)}, u32[]{:S(2)}, u32[]{:S(2)}) %collective-permute-start.3) | collective-permute-done | bytes 65568 | tf_op jit(solution)/shard_map/ppermute | solution.py:285
  18.2 0.0 copy-done
  18.2 0.2 dispatch.1
  18.4 15.9 %all_to_all.10.x_ref = bf16[16,8,1024]{2,1,0:T(8,128)(2,1)S(1)} all-to-all(bf16[16,8,1024]{2,1,0:T(8,128)(2,1)S(1)} %bitcast.11), channel_id=1, replica_groups=mesh['req'=4,'head'=2,'exp'=4] {'req','exp'}, dimensions={0} | all-to-all | bytes 524288 | tf_op jit(solution)/shard_map/all_to_all | solution.py:301
  34.3 0.0 copy-done.1
  34.3 2.2 %expert.1 = bf16[16,8,1024]{2,1,0:T(8,128)(2,1)S(1)} custom-call(bf16[16,8,1024]{2,1,0:T(8,128)(2,1)S(1)} %all_to_all.10.x_ref, f32[1,4096]{1,0:T(1,128)S(1)} %bitcast.12, bf16[4096,768]{1,0:T(8,128)(2,1)S(1)} %get-tuple-element.33.both_ref, bf16[384,4096]{1,0:T(8,128)(2,1)S(1)} %get-tuple-element.34.wd_ref), custom_call_target="tpu_custom_call" | custom-call | tf_op jit(solution)/shard_map/expert/pallas_call | solution.py:230
  36.5 12.8 %all_to_all.11 = bf16[16,8,1024]{2,1,0:T(8,128)(2,1)S(1)} all-to-all(bf16[16,8,1024]{2,1,0:T(8,128)(2,1)S(1)} %expert.1), channel_id=1, replica_groups=mesh['req'=4,'head'=2,'exp'=4] {'req','exp'}, dimensions={0} | all-to-all | bytes 524288 | tf_op jit(solution)/shard_map/all_to_all | solution.py:303
  49.3 0.1 combine.1
  49.5 0.0 collective-permute-start.4
  49.5 1.3 %collective-permute-done.4 = f32[16,1024]{1,0:T(8,128)S(1)} collective-permute-done((f32[16,1024]{1,0:T(8,128)S(1)}, f32[16,1024]{1,0:T(8,128)S(1)}, u32[]{:S(2)}, u32[]{:S(2)}) %collective-permute-start.4) | collective-permute-done | bytes 65568 | tf_op jit(solution)/shard_map/ppermute | solution.py:285
  50.8 0.6 %add_convert_fusion = bf16[16,1024]{1,0:T(8,128)(2,1)} fusion(f32[16,1024]{1,0:T(8,128)S(1)} %get-tuple-element.30, f32[16,1024]{1,0:T(8,128)S(1)} %combine.1, f32[16,1024]{1,0:T(8,128)S(1)} %collective-permute-done.4), kind=kLoop, calls=%fused_computation | loop fusion | flops 49152 | bytes 229376 | tf_op jit(solution)/shard_map/convert_element_type | solution.py:305
Async XLA Ops:
  0.0 8.8 %copy-start.2 = (s32[16,8]{0,1:T(8,128)S(1)}, s32[16,8]{0,1:T(8,128)}, u32[]{:S(2)}) copy-start(s32[16,8]{0,1:T(8,128)} %param.19) | copy-start | bytes 1540
  0.0 8.8 %copy-start.3 = (f32[16,8]{0,1:T(8,128)S(1)}, f32[16,8]{0,1:T(8,128)}, u32[]{:S(2)}) copy-start(f32[16,8]{0,1:T(8,128)} %param.20) | copy-start | bytes 1540
  4.2 5.9 %collective-permute-start.2 = (bf16[4,4096]{1,0:T(4,128)(2,1)S(1)}, bf16[4,4096]{1,0:T(4,128)(2,1)S(1)}, u32[]{:S(2)}, u32[]{:S(2)}) collective-permute-start(bf16[4,4096]{1,0:T(4,128)(2,1)S(1)} %get-tuple-element.23.refs_0_), channel_id=1, source_target_pairs={{0,3},{1,2},{2,1},{3,0},{4,7},{5,6},{6,5},{7,4},{8,11},{9,10},{10,... | collective-permute-start | bytes 98312 | tf_op jit(solution)/shard_map/ppermute | solution.py:290
  8.2 3.9 %collective-permute-start.1 = (bf16[4,4096]{1,0:T(4,128)(2,1)S(1)}, bf16[4,4096]{1,0:T(4,128)(2,1)S(1)}, u32[]{:S(2)}, u32[]{:S(2)}) collective-permute-start(bf16[4,4096]{1,0:T(4,128)(2,1)S(1)} %get-tuple-element.23.refs_0_), channel_id=1, source_target_pairs={{0,2},{1,3},{2,0},{3,1},{4,6},{5,7},{6,4},{7,5},{8,10},{9,11},{10,... | collective-permute-start | bytes 98312 | tf_op jit(solution)/shard_map/ppermute | solution.py:290
  8.7 3.9 %collective-permute-start = (bf16[4,4096]{1,0:T(4,128)(2,1)S(1)}, bf16[4,4096]{1,0:T(4,128)(2,1)S(1)}, u32[]{:S(2)}, u32[]{:S(2)}) collective-permute-start(bf16[4,4096]{1,0:T(4,128)(2,1)S(1)} %get-tuple-element.23.refs_0_), channel_id=1, source_target_pairs={{0,1},{1,0},{2,3},{3,2},{4,5},{5,4},{6,7},{7,6},{8,9},{9,8},{10,11... | collective-permute-start | bytes 98312 | tf_op jit(solution)/shard_map/ppermute | solution.py:290
  12.6 5.6 %copy-start = (bf16[16,1024]{1,0:T(8,128)(2,1)S(1)}, bf16[16,1024]{1,0:T(8,128)(2,1)}, u32[]{:S(2)}) copy-start(bf16[16,1024]{1,0:T(8,128)(2,1)} %resid_ref.1) | copy-start | bytes 98308
  12.6 21.7 %copy-start.1 = (f32[4096]{0:T(1024)S(1)}, f32[4096]{0:T(1024)}, u32[]{:S(2)}) copy-start(f32[4096]{0:T(1024)} %param.18) | copy-start | bytes 49156
  16.9 1.3 %collective-permute-start.3 = (f32[16,1024]{1,0:T(8,128)S(1)}, f32[16,1024]{1,0:T(8,128)S(1)}, u32[]{:S(2)}, u32[]{:S(2)}) collective-permute-start(f32[16,1024]{1,0:T(8,128)S(1)} %get-tuple-element.28.own_ref), channel_id=1, source_target_pairs={{0,4},{4,0},{1,5},{5,1},{2,6},{6,2},{3,7},{7,3},{8,12},{12,8},{9,1... | collective-permute-start | bytes 196616 | tf_op jit(solution)/shard_map/ppermute | solution.py:285
  49.5 1.3 %collective-permute-start.4 = (f32[16,1024]{1,0:T(8,128)S(1)}, f32[16,1024]{1,0:T(8,128)S(1)}, u32[]{:S(2)}, u32[]{:S(2)}) collective-permute-start(f32[16,1024]{1,0:T(8,128)S(1)} %combine.1), channel_id=1, source_target_pairs={{0,4},{4,0},{1,5},{5,1},{2,6},{6,2},{3,7},{7,3},{8,12},{12,8},{9,1... | collective-permute-start | bytes 196616 | tf_op jit(solution)/shard_map/ppermute | solution.py:285

commit v3 on v2

--- a/solution.py
+++ b/solution.py
@@ -38,8 +38,8 @@
         )
 
     ask = pltpu.make_async_copy(q_hbm, q_ref, one.at[0])
-    load = pltpu.make_async_copy(w_hbm, w_ref, one.at[1])
-    span = pltpu.make_async_copy(len_hbm, len_ref, one.at[2])
+    span = pltpu.make_async_copy(len_hbm, len_ref, one.at[1])
+    load = pltpu.make_async_copy(w_hbm.at[pl.ds(0, w_ref.shape[0])], w_ref, one.at[2])
     ask.start()
     span.start()
     for t in range(rows):
@@ -69,7 +69,7 @@
     load.wait()
 
 
-def attend(queries, keys, values, lengths, out_weight):
+def attend(queries, keys, values, lengths, out_weight, early):
     rows, heads, size = queries.shape
     slots, kv_heads = keys.shape[1:3]
     flat = (rows, slots * kv_heads, size)
@@ -77,7 +77,7 @@
         functools.partial(attend_kernel, kv_heads=kv_heads),
         out_shape=(
             pltpu.VMEM((rows, heads * size), BF16),
-            pltpu.VMEM(out_weight.shape, BF16),
+            pltpu.VMEM((early, out_weight.shape[1]), BF16),
         ),
         in_specs=[whole(pltpu.HBM)] * 5,
         out_specs=(whole(), whole()),
@@ -90,14 +90,31 @@
             pltpu.SemaphoreType.DMA((2, rows)),
             pltpu.SemaphoreType.DMA((3,)),
         ],
-        compiler_params=pltpu.CompilerParams(vmem_limit_bytes=16 * 2**20),
+        compiler_params=pltpu.CompilerParams(vmem_limit_bytes=8 * 2**20),
         name="attend",
     )(*map(far, (lengths, queries, keys.reshape(flat), values.reshape(flat), out_weight)))
 
 
-def route_kernel(ids_ref, weight_ref, sel_ref, spread_ref, *, capacity):
+def stage_kernel(
+    ids_hbm, weight_hbm, resid_hbm, gain_hbm, w_hbm,
+    sel_ref, spread_ref, resid_ref, gain_ref, w_ref, ids_ref, weight_ref, sems,
+    *, capacity,
+):
+    tail = w_hbm.at[pl.ds(w_hbm.shape[0] - w_ref.shape[0], w_ref.shape[0])]
+    pairs = (
+        (ids_hbm, ids_ref),
+        (weight_hbm, weight_ref),
+        (tail, w_ref),
+        (resid_hbm, resid_ref),
+        (gain_hbm, gain_ref),
+    )
+    loads = [pltpu.make_async_copy(a, b, sems.at[i]) for i, (a, b) in enumerate(pairs)]
+    for c in loads:
+        c.start()
     total, rows = sel_ref.shape
     experts = total // capacity
+    loads[0].wait()
+    loads[1].wait()
     expert = lax.broadcasted_iota(jnp.int32, (experts, rows), 0)
     chosen = jnp.zeros((experts, rows), F32)
     weight = jnp.zeros((experts, rows), F32)
@@ -115,32 +132,39 @@
     shares = jnp.where(taken, jnp.broadcast_to(weight[:, None, :], seat.shape), 0.0)
     sel_ref[...] = jnp.where(taken, 1.0, 0.0).reshape(total, rows).astype(BF16)
     spread_ref[...] = shares.reshape(total, rows).T
-
-
-def route(expert_ids, route_weights, experts, capacity):
-    rows = expert_ids.shape[0]
+    for c in loads[2:]:
+        c.wait()
+
+
+def stage(expert_ids, route_weights, resid, gain, out_weight, experts, capacity, early):
+    rows, top = expert_ids.shape
     total = experts * capacity
-    return pl.pallas_call(
-        functools.partial(route_kernel, capacity=capacity),
-        out_shape=(pltpu.VMEM((total, rows), BF16), pltpu.VMEM((rows, total), F32)),
-        in_specs=[whole(), whole()],
-        out_specs=(whole(), whole()),
-        compiler_params=pltpu.CompilerParams(vmem_limit_bytes=8 * 2**20),
-        name="route",
-    )(expert_ids.T, route_weights.T)
+    depth, width = out_weight.shape
+    return pl.pallas_call(
+        functools.partial(stage_kernel, capacity=capacity),
+        out_shape=(
+            pltpu.VMEM((total, rows), BF16),
+            pltpu.VMEM((rows, total), F32),
+            pltpu.VMEM(resid.shape, BF16),
+            pltpu.VMEM(gain.shape, F32),
+            pltpu.VMEM((depth - early, width), BF16),
+        ),
+        in_specs=[whole(pltpu.HBM)] * 5,
+        out_specs=(whole(),) * 5,
+        scratch_shapes=[
+            pltpu.VMEM((top, rows), jnp.int32),
+            pltpu.VMEM((top, rows), F32),
+            pltpu.SemaphoreType.DMA((5,)),
+        ],
+        compiler_params=pltpu.CompilerParams(vmem_limit_bytes=8 * 2**20),
+        name="stage",
+    )(*map(far, (expert_ids.T, route_weights.T, resid, gain, out_weight)))
 
 
 def project_kernel(*refs, pieces):
     parts = refs[:pieces]
-    w_ref, wg_hbm, wu_hbm, wd_hbm, o_ref, both_ref, down_ref, sems = refs[pieces:]
-    hid = wg_hbm.shape[1]
-    loads = (
-        pltpu.make_async_copy(wg_hbm, both_ref.at[:, pl.ds(0, hid)], sems.at[0]),
-        pltpu.make_async_copy(wu_hbm, both_ref.at[:, pl.ds(hid, hid)], sems.at[1]),
-        pltpu.make_async_copy(wd_hbm, down_ref, sems.at[2]),
-    )
-    for c in loads:
-        c.start()
+    first_ref, second_ref, o_ref = refs[pieces:]
+    early = first_ref.shape[0]
     loaded = [p[...].astype(F32) for p in parts]
     if pieces > 1:
         place = lax.axis_index("exp")
@@ -153,26 +177,22 @@
         x = jnp.concatenate(blocks, axis=0)
     else:
         x = loaded[0]
-    o_ref[...] = jnp.dot(x.astype(BF16), w_ref[...], preferred_element_type=F32)
-    for c in loads:
-        c.wait()
-
-
-def project(parts, out_weight, w_gate, w_up, w_down, rows):
-    depth, hid = w_gate.shape
+    x = x.astype(BF16)
+    o_ref[...] = jnp.dot(x[:, :early], first_ref[...], preferred_element_type=F32) + jnp.dot(
+        x[:, early:], second_ref[...], preferred_element_type=F32
+    )
+
+
+def project(parts, first, second, rows):
+    width = first.shape[1]
     return pl.pallas_call(
         functools.partial(project_kernel, pieces=len(parts)),
-        out_shape=(
-            pltpu.VMEM((rows, out_weight.shape[1]), F32),
-            pltpu.VMEM((depth, 2 * hid), BF16),
-            pltpu.VMEM(w_down.shape, BF16),
-        ),
-        in_specs=[whole()] * (len(parts) + 1) + [whole(pltpu.HBM)] * 3,
-        out_specs=(whole(),) * 3,
-        scratch_shapes=[pltpu.SemaphoreType.DMA((3,))],
+        out_shape=pltpu.VMEM((rows, width), F32),
+        in_specs=[whole()] * (len(parts) + 2),
+        out_specs=whole(),
         compiler_params=pltpu.CompilerParams(vmem_limit_bytes=8 * 2**20),
         name="project",
-    )(*map(near, parts), near(out_weight), *map(far, (w_gate, w_up, w_down)))
+    )(*map(near, parts), near(first), near(second))
 
 
 def dispatch_kernel(own_ref, other_ref, resid_ref, sel_ref, hid_ref, out_ref):
@@ -196,7 +216,7 @@
     )(near(own), near(other), near(resid), near(selector))
 
 
-def expert_kernel(x_ref, gain_ref, both_ref, wd_ref, o_ref, *, groups, cols):
+def expert_kernel(x_ref, gain_ref, wg_ref, wu_ref, wd_ref, o_ref, *, groups, cols):
     items, width = x_ref.shape[1:]
     depth = cols * width
     hid = wd_ref.shape[0]
@@ -214,7 +234,8 @@
     for e in range(cols):
         sl = slice(e * width, (e + 1) * width)
         normed = (column(e) * inverse * gain_ref[:, sl]).astype(BF16)
-        part = jnp.dot(normed, both_ref[sl, :], preferred_element_type=F32)
+        both = jnp.concatenate([wg_ref[sl, :], wu_ref[sl, :]], axis=1)
+        part = jnp.dot(normed, both, preferred_element_type=F32)
         acc = part if acc is None else acc + part
     gate, up = acc[:, :hid], acc[:, hid:]
     activated = (gate / (1.0 + jnp.exp(-gate)) * up).astype(BF16)
@@ -226,15 +247,15 @@
             o_ref[s * cols + e] = y[s * items : (s + 1) * items, :]
 
 
-def expert(arrived, gain, both, down, groups, cols):
+def expert(arrived, gain, w_gate, w_up, w_down, groups, cols):
     return pl.pallas_call(
         functools.partial(expert_kernel, groups=groups, cols=cols),
         out_shape=pltpu.VMEM(arrived.shape, BF16),
-        in_specs=[whole()] * 4,
+        in_specs=[whole()] * 5,
         out_specs=whole(),
         compiler_params=pltpu.CompilerParams(vmem_limit_bytes=12 * 2**20),
         name="expert",
-    )(*map(near, (arrived, gain, both, down)))
+    )(near(arrived), near(gain), near(w_gate), near(w_up), near(w_down))
 
 
 def combine_kernel(spread_ref, y_ref, o_ref):
@@ -284,7 +305,8 @@
     def swap(x):
         return lax.ppermute(x, "head", [(0, 1), (1, 0)])
 
-    attended, near_weight = attend(queries, keys, values, lengths, out_weight)
+    early = out_weight.shape[0] * 3 // 8
+    attended, first = attend(queries, keys, values, lengths, out_weight, early)
     if exp_count == 4:
         parts = [attended] + [
             lax.ppermute(attended, "exp", [(i, i ^ k) for i in range(exp_count)])
@@ -293,13 +315,18 @@
     else:
         parts = [lax.all_gather(attended, "exp", axis=0, tiled=True)]
 
-    selector, spread = route(expert_ids, route_weights, expert_total, capacity)
-    parts, selector, spread = lax.optimization_barrier((parts, selector, spread))
-    own, both, down = project(parts, near_weight, w_gate[0], w_up[0], w_down[0], group_rows)
-    hidden, outgoing = dispatch(own, swap(own), resid, selector)
+    staged = stage(
+        expert_ids, route_weights, resid, norm_gain[None, :], out_weight, expert_total, capacity, early
+    )
+    parts, staged = lax.optimization_barrier((parts, staged))
+    selector, spread, near_resid, near_gain, second = staged
+    own = project(parts, first, second, group_rows)
+    hidden, outgoing = dispatch(own, swap(own), near_resid, selector)
     outgoing = outgoing.reshape(expert_total, capacity, col_width)
     arrived = lax.all_to_all(outgoing, ("req", "exp"), split_axis=0, concat_axis=0, tiled=True)
-    made = expert(arrived, norm_gain[None, :], both, down, req_count, exp_count)
+    made = expert(
+        arrived, near_gain, w_gate[0], w_up[0], w_down[0], req_count, exp_count
+    )
     returned = lax.all_to_all(made, ("req", "exp"), split_axis=0, concat_axis=0, tiled=True)
     mixture = combine(spread, returned.reshape(expert_total * capacity, col_width))
     return (hidden + (mixture + swap(mixture))).astype(BF16)

time: 51.6 us -> 48.1 us (0.932)
  waiting for transfers between devices: 6.11 us -> 3.59 us
  Pallas kernels: 11.1 us -> 9.93 us
    pallas_call x1, Pallas kernels: 4.24 us -> 1.18 us  [project(): pl.pallas_call(functools.partial(project_kernel, pieces=len(parts)), out_...]
    ppermute x3, waiting for transfers between devices: 3.59 us -> 1.04 us  [local(): lax.ppermute(attended, 'exp', [(i, i ^ k) for i in range(exp_count)])]
    pallas_call x1, Pallas kernels: 0.19 us -> 2.71 us  [stage(): pl.pallas_call(functools.partial(stage_kernel, capacity=capacity), out_sh...]
    pallas_call x1, Pallas kernels: 4.18 us -> 3.48 us  [attend(): pl.pallas_call(functools.partial(attend_kernel, kv_heads=kv_heads), out_s...]
  transfers between devices with their start and end apart: 5 -> 5, of which waited for: 5 -> 4; matrix products, arithmetic and copies ran while one was open for 0% -> 0% of each run, Pallas kernels for 0% -> 6%
where the time goes in v3:
time: 48.1 us; the launch traced here: 47.9 us
  blocking collectives  29.1 us (60%)
  Pallas kernels  9.93 us (21%)
  starting transfers between devices  4.64 us (10%)
  waiting for transfers between devices  3.59 us (7%)
  other arithmetic  0.63 us (1%)
    all_to_all x1, blocking collectives, local(): lax.all_to_all(outgoing, ('req', 'exp'), split_axis=0, concat_axis=0, til...  16.3 us
    all_to_all x1, blocking collectives, local(): lax.all_to_all(made, ('req', 'exp'), split_axis=0, concat_axis=0, tiled=T...  12.8 us
    ppermute x3, starting transfers between devices, local(): lax.ppermute(attended, 'exp', [(i, i ^ k) for i in range(exp_count)])  4.63 us
    pallas_call x1, Pallas kernels, attend(): pl.pallas_call(functools.partial(attend_kernel, kv_heads=kv_heads), out_s...  3.48 us
    pallas_call x1, Pallas kernels, stage(): pl.pallas_call(functools.partial(stage_kernel, capacity=capacity), out_sh...  2.71 us
    ppermute x2, waiting for transfers between devices, swap(): return lax.ppermute(x, 'head', [(0, 1), (1, 0)])  2.55 us
    pallas_call x1, Pallas kernels, expert(): pl.pallas_call(functools.partial(expert_kernel, groups=groups, cols=cols)...  2.21 us
    pallas_call x1, Pallas kernels, project(): pl.pallas_call(functools.partial(project_kernel, pieces=len(parts)), out_...  1.18 us
  transfers between devices with their start and end apart: 5, of which 4 were waited for; matrix products, arithmetic and copies ran while one was open for 0% of the time, Pallas kernels for 6%

profile of v3, /device:TPU:0, one launch (start us, length us, event | category | flops | bytes accessed | tf_op | source)
XLA Modules:
  0.0 47.9 jit_solution(3319142962519710541)
XLA Ops:
  0.0 3.5 %attend.1 = (bf16[4,4096]{1,0:T(4,128)(2,1)S(1)}, bf16[1536,1024]{1,0:T(8,128)(2,1)S(1)}) custom-call(s32[4]{0:T(128)} %len_hbm.1, bf16[4,32,128]{2,1,0:T(8,128)(2,1)} %q_hbm.1, bf16[4,1024,128]{2,1,0:T(8,128)(2,1)} %bitcast.15, bf16[4,1024,128]{2,1,0:T(8,128)(2,1)} %bitcast.16, bf16[4096,1024]{1,0:T(8,128)(2,1)} %w_hbm.3), custom_call_target="tpu_custom_call" | custom-call | tf_op jit(solution)/shard_map/attend/pallas_call | solution.py:76
  3.5 4.0 %collective-permute-start.2 = (bf16[4,4096]{1,0:T(4,128)(2,1)S(1)}, bf16[4,4096]{1,0:T(4,128)(2,1)S(1)}, u32[]{:S(2)}, u32[]{:S(2)}) collective-permute-start(bf16[4,4096]{1,0:T(4,128)(2,1)S(1)} %get-tuple-element.29.refs_0_), channel_id=1, source_target_pairs={{0,3},{1,2},{2,1},{3,0},{4,7},{5,6},{6,5},{7,4},{8,11},{9,10},{10,... | collective-permute-start | bytes 98312 | tf_op jit(solution)/shard_map/ppermute | solution.py:312
  7.5 0.5 %collective-permute-start.1 = (bf16[4,4096]{1,0:T(4,128)(2,1)S(1)}, bf16[4,4096]{1,0:T(4,128)(2,1)S(1)}, u32[]{:S(2)}, u32[]{:S(2)}) collective-permute-start(bf16[4,4096]{1,0:T(4,128)(2,1)S(1)} %get-tuple-element.29.refs_0_), channel_id=1, source_target_pairs={{0,2},{1,3},{2,0},{3,1},{4,6},{5,7},{6,4},{7,5},{8,10},{9,11},{10,... | collective-permute-start | bytes 98312 | tf_op jit(solution)/shard_map/ppermute | solution.py:312
  8.0 0.1 collective-permute-start
  8.1 0.0 copy-start.2
  8.1 2.7 %stage.1 = (bf16[128,16]{1,0:T(8,128)(2,1)S(1)}, f32[16,128]{1,0:T(8,128)S(1)}, bf16[16,1024]{1,0:T(8,128)(2,1)S(1)}, f32[1,4096]{1,0:T(1,128)S(1)}, bf16[2560,1024]{1,0:T(8,128)(2,1)S(1)}) custom-call(s32[8,16]{1,0:T(8,128)} %bitcast.18, f32[8,16]{1,0:T(8,128)} %bitcast.19, bf16[16,1024]{1,0:T(8,128)(2,1)} %resid_hbm.1, f32[1,4096]{1,0:T(1,128)} %bitcast.17, ...), custom_call_target="tpu_custom_call" | custom-call | tf_op jit(solution)/shard_map/stage/pallas_call | solution.py:143
  10.8 0.0 collective-permute-done.2.refs_3_
  10.9 0.5 %collective-permute-done.1.refs_2_ = bf16[4,4096]{1,0:T(4,128)(2,1)S(1)} collective-permute-done((bf16[4,4096]{1,0:T(4,128)(2,1)S(1)}, bf16[4,4096]{1,0:T(4,128)(2,1)S(1)}, u32[]{:S(2)}, u32[]{:S(2)}) %collective-permute-start.1) | collective-permute-done | bytes 32800 | tf_op jit(solution)/shard_map/ppermute | solution.py:312
  11.4 0.5 %collective-permute-done.refs_1_ = bf16[4,4096]{1,0:T(4,128)(2,1)S(1)} collective-permute-done((bf16[4,4096]{1,0:T(4,128)(2,1)S(1)}, bf16[4,4096]{1,0:T(4,128)(2,1)S(1)}, u32[]{:S(2)}, u32[]{:S(2)}) %collective-permute-start) | collective-permute-done | bytes 32800 | tf_op jit(solution)/shard_map/ppermute | solution.py:312
  11.9 0.0 copy-start
  11.9 0.0 copy-start.1
  11.9 1.2 %project.1.own_ref = f32[16,1024]{1,0:T(8,128)S(1)} custom-call(bf16[4,4096]{1,0:T(4,128)(2,1)S(1)} %get-tuple-element.29.refs_0_, bf16[4,4096]{1,0:T(4,128)(2,1)S(1)} %collective-permute-done.refs_1_, bf16[4,4096]{1,0:T(4,128)(2,1)S(1)} %collective-permute-done.1.refs_2_, bf16[4,4096]{1,0:T(4,128)(2,1)S(1)} %collective-permute-done.2.refs_3_, ...), custom_call_target="tpu_custom_call" | custom-call | tf_op jit(solution)/shard_map/project/pallas_call | solution.py:188
  13.1 0.0 collective-permute-start.3
  13.1 1.3 %collective-permute-done.3.other_ref = f32[16,1024]{1,0:T(8,128)S(1)} collective-permute-done((f32[16,1024]{1,0:T(8,128)S(1)}, f32[16,1024]{1,0:T(8,128)S(1)}, u32[]{:S(2)}, u32[]{:S(2)}) %collective-permute-start.3) | collective-permute-done | bytes 65568 | tf_op jit(solution)/shard_map/ppermute | solution.py:306
  14.4 0.2 dispatch.1
  14.6 16.3 %all_to_all.10.x_ref = bf16[16,8,1024]{2,1,0:T(8,128)(2,1)S(1)} all-to-all(bf16[16,8,1024]{2,1,0:T(8,128)(2,1)S(1)} %bitcast.14), channel_id=1, replica_groups=mesh['req'=4,'head'=2,'exp'=4] {'req','exp'}, dimensions={0} | all-to-all | bytes 524288 | tf_op jit(solution)/shard_map/all_to_all | solution.py:326
  30.8 0.0 copy-done.2
  30.8 0.0 copy-done
  30.8 0.0 copy-done.1
  30.8 2.2 %expert.1 = bf16[16,8,1024]{2,1,0:T(8,128)(2,1)S(1)} custom-call(bf16[16,8,1024]{2,1,0:T(8,128)(2,1)S(1)} %all_to_all.10.x_ref, f32[1,4096]{1,0:T(1,128)S(1)} %get-tuple-element.40.gain_ref, bf16[4096,384]{1,0:T(8,128)(2,1)S(1)} %bitcast.10, bf16[4096,384]{1,0:T(8,128)(2,1)S(1)} %bitcast.11, bf16[384,4096]{1,0:T(8,128)(2,1)S(1)} %bitcast.12), custom_call_target="tpu_custom_call" | custom-call | tf_op jit(solution)/shard_map/expert/pallas_call | solution.py:251
  33.0 12.8 %all_to_all.11 = bf16[16,8,1024]{2,1,0:T(8,128)(2,1)S(1)} all-to-all(bf16[16,8,1024]{2,1,0:T(8,128)(2,1)S(1)} %expert.1), channel_id=1, replica_groups=mesh['req'=4,'head'=2,'exp'=4] {'req','exp'}, dimensions={0} | all-to-all | bytes 524288 | tf_op jit(solution)/shard_map/all_to_all | solution.py:330
  45.8 0.1 combine.1
  46.0 0.0 collective-permute-start.4
  46.0 1.3 %collective-permute-done.4 = f32[16,1024]{1,0:T(8,128)S(1)} collective-permute-done((f32[16,1024]{1,0:T(8,128)S(1)}, f32[16,1024]{1,0:T(8,128)S(1)}, u32[]{:S(2)}, u32[]{:S(2)}) %collective-permute-start.4) | collective-permute-done | bytes 65568 | tf_op jit(solution)/shard_map/ppermute | solution.py:306
  47.3 0.6 %add_convert_fusion = bf16[16,1024]{1,0:T(8,128)(2,1)} fusion(f32[16,1024]{1,0:T(8,128)S(1)} %get-tuple-element.37, f32[16,1024]{1,0:T(8,128)S(1)} %combine.1, f32[16,1024]{1,0:T(8,128)S(1)} %collective-permute-done.4), kind=kLoop, calls=%fused_computation | loop fusion | flops 49152 | bytes 229376 | tf_op jit(solution)/shard_map/convert_element_type | solution.py:332
Async XLA Ops:
  3.5 7.4 %collective-permute-start.2 = (bf16[4,4096]{1,0:T(4,128)(2,1)S(1)}, bf16[4,4096]{1,0:T(4,128)(2,1)S(1)}, u32[]{:S(2)}, u32[]{:S(2)}) collective-permute-start(bf16[4,4096]{1,0:T(4,128)(2,1)S(1)} %get-tuple-element.29.refs_0_), channel_id=1, source_target_pairs={{0,3},{1,2},{2,1},{3,0},{4,7},{5,6},{6,5},{7,4},{8,11},{9,10},{10,... | collective-permute-start | bytes 98312 | tf_op jit(solution)/shard_map/ppermute | solution.py:312
  7.5 3.9 %collective-permute-start.1 = (bf16[4,4096]{1,0:T(4,128)(2,1)S(1)}, bf16[4,4096]{1,0:T(4,128)(2,1)S(1)}, u32[]{:S(2)}, u32[]{:S(2)}) collective-permute-start(bf16[4,4096]{1,0:T(4,128)(2,1)S(1)} %get-tuple-element.29.refs_0_), channel_id=1, source_target_pairs={{0,2},{1,3},{2,0},{3,1},{4,6},{5,7},{6,4},{7,5},{8,10},{9,11},{10,... | collective-permute-start | bytes 98312 | tf_op jit(solution)/shard_map/ppermute | solution.py:312
  8.0 3.9 %collective-permute-start = (bf16[4,4096]{1,0:T(4,128)(2,1)S(1)}, bf16[4,4096]{1,0:T(4,128)(2,1)S(1)}, u32[]{:S(2)}, u32[]{:S(2)}) collective-permute-start(bf16[4,4096]{1,0:T(4,128)(2,1)S(1)} %get-tuple-element.29.refs_0_), channel_id=1, source_target_pairs={{0,1},{1,0},{2,3},{3,2},{4,5},{5,4},{6,7},{7,6},{8,9},{9,8},{10,11... | collective-permute-start | bytes 98312 | tf_op jit(solution)/shard_map/ppermute | solution.py:312
  8.1 22.7 %copy-start.2 = (bf16[1,384,4096]{2,1,0:T(8,128)(2,1)S(1)}, bf16[1,384,4096]{2,1,0:T(8,128)(2,1)}, u32[]{:S(2)}) copy-start(bf16[1,384,4096]{2,1,0:T(8,128)(2,1)} %param.23) | copy-start | bytes 9437188
  11.9 18.9 %copy-start = (bf16[1,4096,384]{2,1,0:T(8,128)(2,1)S(1)}, bf16[1,4096,384]{2,1,0:T(8,128)(2,1)}, u32[]{:S(2)}) copy-start(bf16[1,4096,384]{2,1,0:T(8,128)(2,1)} %param.21) | copy-start | bytes 9437188
  11.9 18.9 %copy-start.1 = (bf16[1,4096,384]{2,1,0:T(8,128)(2,1)S(1)}, bf16[1,4096,384]{2,1,0:T(8,128)(2,1)}, u32[]{:S(2)}) copy-start(bf16[1,4096,384]{2,1,0:T(8,128)(2,1)} %param.22) | copy-start | bytes 9437188
  13.1 1.3 %collective-permute-start.3 = (f32[16,1024]{1,0:T(8,128)S(1)}, f32[16,1024]{1,0:T(8,128)S(1)}, u32[]{:S(2)}, u32[]{:S(2)}) collective-permute-start(f32[16,1024]{1,0:T(8,128)S(1)} %project.1.own_ref), channel_id=1, source_target_pairs={{0,4},{4,0},{1,5},{5,1},{2,6},{6,2},{3,7},{7,3},{8,12},{12,8},{9,1... | collective-permute-start | bytes 196616 | tf_op jit(solution)/shard_map/ppermute | solution.py:306
  46.0 1.3 %collective-permute-start.4 = (f32[16,1024]{1,0:T(8,128)S(1)}, f32[16,1024]{1,0:T(8,128)S(1)}, u32[]{:S(2)}, u32[]{:S(2)}) collective-permute-start(f32[16,1024]{1,0:T(8,128)S(1)} %combine.1), channel_id=1, source_target_pairs={{0,4},{4,0},{1,5},{5,1},{2,6},{6,2},{3,7},{7,3},{8,12},{12,8},{9,1... | collective-permute-start | bytes 196616 | tf_op jit(solution)/shard_map/ppermute | solution.py:306

commit v4 on v3

--- a/solution.py
+++ b/solution.py
@@ -29,41 +29,65 @@
     *, kv_heads
 ):
     rows, heads, size = q_ref.shape
+    width = kbuf.shape[1]
     per = heads // kv_heads
-
-    def copies(t):
-        return (
-            pltpu.make_async_copy(k_hbm.at[t], kbuf.at[t], sems.at[0, t]),
-            pltpu.make_async_copy(v_hbm.at[t], vbuf.at[t], sems.at[1, t]),
-        )
-
+    tile = 128
+    tiles = width // tile
     ask = pltpu.make_async_copy(q_hbm, q_ref, one.at[0])
     span = pltpu.make_async_copy(len_hbm, len_ref, one.at[1])
     load = pltpu.make_async_copy(w_hbm.at[pl.ds(0, w_ref.shape[0])], w_ref, one.at[2])
-    ask.start()
-    span.start()
-    for t in range(rows):
-        for c in copies(t):
-            c.start()
-    load.start()
-    width = kbuf.shape[1]
-    col = lax.broadcasted_iota(jnp.int32, (heads, width), 1)
-    row = lax.broadcasted_iota(jnp.int32, (heads, width), 0)
-    same = (col % kv_heads) == (row // per)
-    slot = jnp.where(same, col // kv_heads, jnp.int32(2**30))
+    kcs = [pltpu.make_async_copy(k_hbm.at[t], kbuf.at[t], sems.at[0, t]) for t in range(rows)]
+    vcs = [pltpu.make_async_copy(v_hbm.at[t], vbuf.at[t], sems.at[1, t]) for t in range(rows)]
+    for c in [ask, span] + kcs + vcs + [load]:
+        c.start()
+    lane = lax.broadcasted_iota(jnp.int32, (per, tile), 1)
+    group = lane % kv_heads
+    slot = lane // kv_heads
+    rate = math.log2(math.e) / math.sqrt(size)
+
+    def grouped(fold, unit, reduce):
+        res = jnp.zeros((per, tile), F32)
+        for g in range(kv_heads):
+            one_g = reduce(jnp.where(group == g, fold, unit), axis=1, keepdims=True)
+            res = jnp.where(group == g, one_g, res)
+        return res
+
     ask.wait()
     span.wait()
+    for c in kcs:
+        c.wait()
+    weights = []
     for t in range(rows):
-        kc, vc = copies(t)
-        kc.wait()
-        logits = lax.dot_general(
+        full = lax.dot_general(
             q_ref[t], kbuf[t], (((1,), (1,)), ((), ())), preferred_element_type=F32
-        ) * (1.0 / math.sqrt(size))
-        logits = jnp.where(slot < len_ref[t], logits, -1e30)
-        raised = jnp.exp(logits - jnp.max(logits, axis=1, keepdims=True))
-        weights = (raised / jnp.sum(raised, axis=1, keepdims=True)).astype(BF16)
-        vc.wait()
-        scr[t * heads : (t + 1) * heads, :] = jnp.dot(weights, vbuf[t], preferred_element_type=F32)
+        )
+        parts = []
+        for i in range(tiles):
+            cut = slice(i * tile, (i + 1) * tile)
+            mine = full[:per, cut]
+            for g in range(1, kv_heads):
+                mine = jnp.where(group == g, full[g * per : (g + 1) * per, cut], mine)
+            live = slot < len_ref[t] - i * (tile // kv_heads)
+            parts.append(jnp.where(live, mine, -1e30))
+        top = grouped(functools.reduce(jnp.maximum, parts), -1e30, jnp.max)
+        raised = [jnp.exp2((p - top) * rate) for p in parts]
+        share = 1.0 / grouped(functools.reduce(jnp.add, raised), 0.0, jnp.sum)
+        soft = [(r * share).astype(BF16) for r in raised]
+        weights.append(
+            jnp.concatenate(
+                [
+                    jnp.concatenate([jnp.where(group == g, w, jnp.zeros_like(w)) for w in soft], axis=1)
+                    for g in range(kv_heads)
+                ],
+                axis=0,
+            )
+        )
+    for c in vcs:
+        c.wait()
+    for t in range(rows):
+        scr[t * heads : (t + 1) * heads, :] = jnp.dot(
+            weights[t], vbuf[t], preferred_element_type=F32
+        )
     for j in range(heads):
         o_ref[:, j * size : (j + 1) * size] = scr[pl.ds(j, rows, stride=heads), :].astype(BF16)
     load.wait()
@@ -163,7 +187,7 @@
 
 def project_kernel(*refs, pieces):
     parts = refs[:pieces]
-    first_ref, second_ref, o_ref = refs[pieces:]
+    first_ref, second_ref, keep_ref, give_ref = refs[pieces:]
     early = first_ref.shape[0]
     loaded = [p[...].astype(F32) for p in parts]
     if pieces > 1:
@@ -178,36 +202,42 @@
     else:
         x = loaded[0]
     x = x.astype(BF16)
-    o_ref[...] = jnp.dot(x[:, :early], first_ref[...], preferred_element_type=F32) + jnp.dot(
+    res = jnp.dot(x[:, :early], first_ref[...], preferred_element_type=F32) + jnp.dot(
         x[:, early:], second_ref[...], preferred_element_type=F32
     )
+    half = keep_ref.shape[1]
+    low = lax.axis_index("head") == 0
+    keep_ref[...] = jnp.where(low, res[:, :half], res[:, half:])
+    give_ref[...] = jnp.where(low, res[:, half:], res[:, :half])
 
 
 def project(parts, first, second, rows):
-    width = first.shape[1]
+    half = first.shape[1] // 2
     return pl.pallas_call(
         functools.partial(project_kernel, pieces=len(parts)),
-        out_shape=pltpu.VMEM((rows, width), F32),
+        out_shape=(pltpu.VMEM((rows, half), F32),) * 2,
         in_specs=[whole()] * (len(parts) + 2),
-        out_specs=whole(),
+        out_specs=(whole(), whole()),
         compiler_params=pltpu.CompilerParams(vmem_limit_bytes=8 * 2**20),
         name="project",
     )(*map(near, parts), near(first), near(second))
 
 
 def dispatch_kernel(own_ref, other_ref, resid_ref, sel_ref, hid_ref, out_ref):
-    hidden = resid_ref[...].astype(F32) + (own_ref[...] + other_ref[...])
+    half = own_ref.shape[1]
+    resid = jnp.where(lax.axis_index("head") == 0, resid_ref[:, :half], resid_ref[:, half:])
+    hidden = resid.astype(F32) + (own_ref[...] + other_ref[...])
     hid_ref[...] = hidden
     out_ref[...] = jnp.dot(sel_ref[...], hidden.astype(BF16), preferred_element_type=F32).astype(BF16)
 
 
 def dispatch(own, other, resid, selector):
-    rows, width = resid.shape
+    rows, half = own.shape
     return pl.pallas_call(
         dispatch_kernel,
         out_shape=(
-            pltpu.VMEM((rows, width), F32),
-            pltpu.VMEM((selector.shape[0], width), BF16),
+            pltpu.VMEM((rows, half), F32),
+            pltpu.VMEM((selector.shape[0], half), BF16),
         ),
         in_specs=[whole()] * 4,
         out_specs=(whole(), whole()),
@@ -216,49 +246,77 @@
     )(near(own), near(other), near(resid), near(selector))
 
 
-def expert_kernel(x_ref, gain_ref, wg_ref, wu_ref, wd_ref, o_ref, *, groups, cols):
-    items, width = x_ref.shape[1:]
-    depth = cols * width
+def expert_kernel(
+    own_ref, other_ref, gain_ref, wg_ref, wu_ref, wd_ref, keep_ref, give_ref, *, groups, cols
+):
+    items, half = own_ref.shape[1:]
+    depth = 2 * cols * half
     hid = wd_ref.shape[0]
-
-    def column(e):
-        return jnp.concatenate([x_ref[s * cols + e].astype(F32) for s in range(groups)], axis=0)
+    low = lax.axis_index("head") == 0
+
+    def column(e, lower):
+        picks = []
+        for s in range(groups):
+            a = own_ref[s * cols + e].astype(F32)
+            b = other_ref[s * cols + e].astype(F32)
+            picks.append(jnp.where(low, a, b) if lower else jnp.where(low, b, a))
+        return jnp.concatenate(picks, axis=0)
 
     squares = None
     for e in range(cols):
-        x = column(e)
-        part = jnp.sum(x * x, axis=1, keepdims=True)
-        squares = part if squares is None else squares + part
+        for lower in (True, False):
+            x = column(e, lower)
+            part = jnp.sum(x * x, axis=1, keepdims=True)
+            squares = part if squares is None else squares + part
     inverse = lax.rsqrt(squares / depth + 1e-06)
     acc = None
     for e in range(cols):
-        sl = slice(e * width, (e + 1) * width)
-        normed = (column(e) * inverse * gain_ref[:, sl]).astype(BF16)
-        both = jnp.concatenate([wg_ref[sl, :], wu_ref[sl, :]], axis=1)
-        part = jnp.dot(normed, both, preferred_element_type=F32)
-        acc = part if acc is None else acc + part
+        for i, lower in enumerate((True, False)):
+            sl = slice((2 * e + i) * half, (2 * e + i + 1) * half)
+            normed = (column(e, lower) * inverse * gain_ref[:, sl]).astype(BF16)
+            both = jnp.concatenate([wg_ref[sl, :], wu_ref[sl, :]], axis=1)
+            part = jnp.dot(normed, both, preferred_element_type=F32)
+            acc = part if acc is None else acc + part
     gate, up = acc[:, :hid], acc[:, hid:]
     activated = (gate / (1.0 + jnp.exp(-gate)) * up).astype(BF16)
     for e in range(cols):
         y = jnp.dot(
-            activated, wd_ref[:, e * width : (e + 1) * width], preferred_element_type=F32
-        ).astype(BF16)
+            activated, wd_ref[:, 2 * e * half : 2 * (e + 1) * half], preferred_element_type=F32
+        )
+        keep = jnp.where(low, y[:, :half], y[:, half:])
+        give = jnp.where(low, y[:, half:], y[:, :half]).astype(BF16)
         for s in range(groups):
-            o_ref[s * cols + e] = y[s * items : (s + 1) * items, :]
-
-
-def expert(arrived, gain, w_gate, w_up, w_down, groups, cols):
+            keep_ref[s * cols + e] = keep[s * items : (s + 1) * items, :]
+            give_ref[s * cols + e] = give[s * items : (s + 1) * items, :]
+
+
+def expert(own, other, gain, w_gate, w_up, w_down, groups, cols):
     return pl.pallas_call(
         functools.partial(expert_kernel, groups=groups, cols=cols),
-        out_shape=pltpu.VMEM(arrived.shape, BF16),
-        in_specs=[whole()] * 5,
-        out_specs=whole(),
+        out_shape=(pltpu.VMEM(own.shape, F32), pltpu.VMEM(own.shape, BF16)),
+        in_specs=[whole()] * 6,
+        out_specs=(whole(), whole()),
         compiler_params=pltpu.CompilerParams(vmem_limit_bytes=12 * 2**20),
         name="expert",
-    )(near(arrived), near(gain), near(w_gate), near(w_up), near(w_down))
-
-
-def combine_kernel(spread_ref, y_ref, o_ref):
+    )(*map(near, (own, other, gain, w_gate, w_up, w_down)))
+
+
+def merge_kernel(keep_ref, got_ref, o_ref):
+    o_ref[...] = (keep_ref[...] + got_ref[...].astype(F32)).astype(BF16)
+
+
+def merge(keep, got):
+    return pl.pallas_call(
+        merge_kernel,
+        out_shape=pltpu.VMEM(keep.shape, BF16),
+        in_specs=[whole(), whole()],
+        out_specs=whole(),
+        compiler_params=pltpu.CompilerParams(vmem_limit_bytes=8 * 2**20),
+        name="merge",
+    )(near(keep), near(got))
+
+
+def combine_kernel(spread_ref, y_ref, hid_ref, o_ref):
     rows = spread_ref.shape[0]
     spread = spread_ref[...]
     high = spread.astype(BF16)
@@ -267,18 +325,38 @@
     low = (rest - mid.astype(F32)).astype(BF16)
     stacked = jnp.concatenate([high, mid, low], axis=0)
     res = jnp.dot(stacked, y_ref[...], preferred_element_type=F32)
-    o_ref[...] = res[:rows] + (res[rows : 2 * rows] + res[2 * rows :])
-
-
-def combine(spread, returned):
+    mixture = res[:rows] + (res[rows : 2 * rows] + res[2 * rows :])
+    o_ref[...] = (hid_ref[...] + mixture).astype(BF16)
+
+
+def combine(spread, returned, hidden):
     return pl.pallas_call(
         combine_kernel,
-        out_shape=pltpu.VMEM((spread.shape[0], returned.shape[1]), F32),
+        out_shape=pltpu.VMEM(hidden.shape, BF16),
+        in_specs=[whole()] * 3,
+        out_specs=whole(),
+        compiler_params=pltpu.CompilerParams(vmem_limit_bytes=8 * 2**20),
+        name="combine",
+    )(near(spread), near(returned), near(hidden))
+
+
+def join_kernel(own_ref, other_ref, o_ref):
+    half = own_ref.shape[1]
+    low = lax.axis_index("head") == 0
+    o_ref[:, :half] = jnp.where(low, own_ref[...], other_ref[...])
+    o_ref[:, half:] = jnp.where(low, other_ref[...], own_ref[...])
+
+
+def join(own, other):
+    rows, half = own.shape
+    return pl.pallas_call(
+        join_kernel,
+        out_shape=jax.ShapeDtypeStruct((rows, 2 * half), BF16),
         in_specs=[whole(), whole()],
         out_specs=whole(),
         compiler_params=pltpu.CompilerParams(vmem_limit_bytes=8 * 2**20),
-        name="combine",
-    )(near(spread), near(returned))
+        name="join",
+    )(near(own), near(other))
 
 
 def local(
@@ -298,7 +376,7 @@
     req_count = lax.axis_size("req")
     exp_count = lax.axis_size("exp")
     rows_dev = queries.shape[0]
-    group_rows, col_width = resid.shape
+    group_rows = resid.shape[0]
     capacity = 2 * rows_dev
     expert_total = req_count * exp_count
 
@@ -320,16 +398,20 @@
     )
     parts, staged = lax.optimization_barrier((parts, staged))
     selector, spread, near_resid, near_gain, second = staged
-    own = project(parts, first, second, group_rows)
-    hidden, outgoing = dispatch(own, swap(own), near_resid, selector)
-    outgoing = outgoing.reshape(expert_total, capacity, col_width)
-    arrived = lax.all_to_all(outgoing, ("req", "exp"), split_axis=0, concat_axis=0, tiled=True)
-    made = expert(
-        arrived, near_gain, w_gate[0], w_up[0], w_down[0], req_count, exp_count
+    keep, give = project(parts, first, second, group_rows)
+    hidden, outgoing = dispatch(keep, swap(give), near_resid, selector)
+    half = hidden.shape[1]
+
+    def exchange(x):
+        return lax.all_to_all(x, ("req", "exp"), split_axis=0, concat_axis=0, tiled=True)
+
+    arrived = exchange(outgoing.reshape(expert_total, capacity, half))
+    keep, give = expert(
+        arrived, swap(arrived), near_gain, w_gate[0], w_up[0], w_down[0], req_count, exp_count
     )
-    returned = lax.all_to_all(made, ("req", "exp"), split_axis=0, concat_axis=0, tiled=True)
-    mixture = combine(spread, returned.reshape(expert_total * capacity, col_width))
-    return (hidden + (mixture + swap(mixture))).astype(BF16)
+    returned = exchange(merge(keep, swap(give)))
+    mine = combine(spread, returned.reshape(expert_total * capacity, half), hidden)
+    return join(mine, swap(mine))
 
 
 def solution(mesh):

time: 48.1 us -> 45.4 us (0.944)
  blocking collectives: 29.1 us -> 24.6 us
  waiting for transfers between devices: 3.59 us -> 6.01 us
  other arithmetic: 0.63 us -> 0 us
    all_to_all x2, blocking collectives: 29.1 us -> 24.6 us  [exchange(): lax.all_to_all(x, ('req', 'exp'), split_axis=0, concat_axis=0, tiled=True)]
    ppermute x2 -> x4, waiting for transfers between devices: 2.55 us -> 4.96 us  [swap(): return lax.ppermute(x, 'head', [(0, 1), (1, 0)])]
    pallas_call x1, Pallas kernels: 3.48 us -> 2.65 us  [attend(): pl.pallas_call(functools.partial(attend_kernel, kv_heads=kv_heads), out_s...]
    convert_element_type x1 -> x0, other arithmetic: 0.63 us -> none  [local(): return (hidden + (mixture + swap(mixture))).astype(BF16)]
    pallas_call x2 -> x4, Pallas kernels: 0.34 us -> 0.94 us  [the longest x1 0.62 us: join(): pl.pallas_call(join_kernel, out_shape=jax.ShapeDtypeStruct((rows, 2 * hal...]
  transfers between devices with their start and end apart: 5 -> 7, of which waited for: 4 -> 6; matrix products, arithmetic and copies ran while one was open for 0% -> 0% of each run, Pallas kernels for 6% -> 6%
where the time goes in v4:
time: 45.4 us; the launch traced here: 45.2 us
  blocking collectives  24.6 us (54%)
  Pallas kernels  9.64 us (21%)
  waiting for transfers between devices  6.01 us (13%)
  starting transfers between devices  4.85 us (11%)
    all_to_all x2, blocking collectives, exchange(): lax.all_to_all(x, ('req', 'exp'), split_axis=0, concat_axis=0, tiled=True)  24.6 us
    ppermute x4, waiting for transfers between devices, swap(): return lax.ppermute(x, 'head', [(0, 1), (1, 0)])  4.96 us
    ppermute x3, starting transfers between devices, local(): lax.ppermute(attended, 'exp', [(i, i ^ k) for i in range(exp_count)])  4.63 us
    pallas_call x1, Pallas kernels, stage(): pl.pallas_call(functools.partial(stage_kernel, capacity=capacity), out_sh...  2.71 us
    pallas_call x1, Pallas kernels, attend(): pl.pallas_call(functools.partial(attend_kernel, kv_heads=kv_heads), out_s...  2.65 us
    pallas_call x1, Pallas kernels, expert(): pl.pallas_call(functools.partial(expert_kernel, groups=groups, cols=cols)...  2.14 us
    pallas_call x1, Pallas kernels, project(): pl.pallas_call(functools.partial(project_kernel, pieces=len(parts)), out_...  1.19 us
    ppermute x3, waiting for transfers between devices, local(): lax.ppermute(attended, 'exp', [(i, i ^ k) for i in range(exp_count)])  1.05 us
  transfers between devices with their start and end apart: 7, of which 6 were waited for; matrix products, arithmetic and copies ran while one was open for 0% of the time, Pallas kernels for 6%

profile of v4, /device:TPU:0, one launch (start us, length us, event | category | flops | bytes accessed | tf_op | source)
XLA Modules:
  0.0 45.2 jit_solution(12029571467623501897)
XLA Ops:
  0.0 2.7 %attend.1 = (bf16[4,4096]{1,0:T(4,128)(2,1)S(1)}, bf16[1536,1024]{1,0:T(8,128)(2,1)S(1)}) custom-call(s32[4]{0:T(128)} %len_hbm.1, bf16[4,32,128]{2,1,0:T(8,128)(2,1)} %q_hbm.1, bf16[4,1024,128]{2,1,0:T(8,128)(2,1)} %bitcast.15, bf16[4,1024,128]{2,1,0:T(8,128)(2,1)} %bitcast.16, bf16[4096,1024]{1,0:T(8,128)(2,1)} %w_hbm.3), custom_call_target="tpu_custom_call" | custom-call | tf_op jit(solution)/shard_map/attend/pallas_call | solution.py:100
  2.7 4.0 %collective-permute-start.2 = (bf16[4,4096]{1,0:T(4,128)(2,1)S(1)}, bf16[4,4096]{1,0:T(4,128)(2,1)S(1)}, u32[]{:S(2)}, u32[]{:S(2)}) collective-permute-start(bf16[4,4096]{1,0:T(4,128)(2,1)S(1)} %get-tuple-element.34.refs_0_), channel_id=1, source_target_pairs={{0,3},{1,2},{2,1},{3,0},{4,7},{5,6},{6,5},{7,4},{8,11},{9,10},{10,... | collective-permute-start | bytes 98312 | tf_op jit(solution)/shard_map/ppermute | solution.py:390
  6.7 0.5 %collective-permute-start.1 = (bf16[4,4096]{1,0:T(4,128)(2,1)S(1)}, bf16[4,4096]{1,0:T(4,128)(2,1)S(1)}, u32[]{:S(2)}, u32[]{:S(2)}) collective-permute-start(bf16[4,4096]{1,0:T(4,128)(2,1)S(1)} %get-tuple-element.34.refs_0_), channel_id=1, source_target_pairs={{0,2},{1,3},{2,0},{3,1},{4,6},{5,7},{6,4},{7,5},{8,10},{9,11},{10,... | collective-permute-start | bytes 98312 | tf_op jit(solution)/shard_map/ppermute | solution.py:390
  7.2 0.1 collective-permute-start
  7.3 0.0 copy-start.2
  7.3 2.7 %stage.1 = (bf16[128,16]{1,0:T(8,128)(2,1)S(1)}, f32[16,128]{1,0:T(8,128)S(1)}, bf16[16,1024]{1,0:T(8,128)(2,1)S(1)}, f32[1,4096]{1,0:T(1,128)S(1)}, bf16[2560,1024]{1,0:T(8,128)(2,1)S(1)}) custom-call(s32[8,16]{1,0:T(8,128)} %bitcast.18, f32[8,16]{1,0:T(8,128)} %bitcast.19, bf16[16,1024]{1,0:T(8,128)(2,1)} %resid_hbm.1, f32[1,4096]{1,0:T(1,128)} %bitcast.17, ...), custom_call_target="tpu_custom_call" | custom-call | tf_op jit(solution)/shard_map/stage/pallas_call | solution.py:167
  10.0 0.0 collective-permute-done.2.refs_3_
  10.0 0.5 %collective-permute-done.1.refs_2_ = bf16[4,4096]{1,0:T(4,128)(2,1)S(1)} collective-permute-done((bf16[4,4096]{1,0:T(4,128)(2,1)S(1)}, bf16[4,4096]{1,0:T(4,128)(2,1)S(1)}, u32[]{:S(2)}, u32[]{:S(2)}) %collective-permute-start.1) | collective-permute-done | bytes 32800 | tf_op jit(solution)/shard_map/ppermute | solution.py:390
  10.6 0.5 %collective-permute-done.refs_1_ = bf16[4,4096]{1,0:T(4,128)(2,1)S(1)} collective-permute-done((bf16[4,4096]{1,0:T(4,128)(2,1)S(1)}, bf16[4,4096]{1,0:T(4,128)(2,1)S(1)}, u32[]{:S(2)}, u32[]{:S(2)}) %collective-permute-start) | collective-permute-done | bytes 32800 | tf_op jit(solution)/shard_map/ppermute | solution.py:390
  11.1 0.0 copy-start
  11.1 0.0 copy-start.1
  11.1 1.2 %project.1 = (f32[16,512]{1,0:T(8,128)S(1)}, f32[16,512]{1,0:T(8,128)S(1)}) custom-call(bf16[4,4096]{1,0:T(4,128)(2,1)S(1)} %get-tuple-element.34.refs_0_, bf16[4,4096]{1,0:T(4,128)(2,1)S(1)} %collective-permute-done.refs_1_, bf16[4,4096]{1,0:T(4,128)(2,1)S(1)} %collective-permute-done.1.refs_2_, bf16[4,4096]{1,0:T(4,128)(2,1)S(1)} %collective-permute-done.2.refs_3_, ...), custom_call_target="tpu_custom_call" | custom-call | tf_op jit(solution)/shard_map/project/pallas_call | solution.py:216
  12.3 0.0 collective-permute-start.3
  12.3 1.2 %collective-permute-done.3.other_ref = f32[16,512]{1,0:T(8,128)S(1)} collective-permute-done((f32[16,512]{1,0:T(8,128)S(1)}, f32[16,512]{1,0:T(8,128)S(1)}, u32[]{:S(2)}, u32[]{:S(2)}) %collective-permute-start.3) | collective-permute-done | bytes 32800 | tf_op jit(solution)/shard_map/ppermute | solution.py:384
  13.5 0.2 dispatch.1
  13.7 13.9 %all_to_all.10.own_ref = bf16[16,8,512]{2,1,0:T(8,128)(2,1)S(1)} all-to-all(bf16[16,8,512]{2,1,0:T(8,128)(2,1)S(1)} %bitcast.14), channel_id=1, replica_groups=mesh['req'=4,'head'=2,'exp'=4] {'req','exp'}, dimensions={0} | all-to-all | bytes 262144 | tf_op jit(solution)/shard_map/all_to_all | solution.py:406
  27.5 0.0 collective-permute-start.4
  27.5 1.3 %collective-permute-done.4.other_ref = bf16[16,8,512]{2,1,0:T(8,128)(2,1)S(1)} collective-permute-done((bf16[16,8,512]{2,1,0:T(8,128)(2,1)S(1)}, bf16[16,8,512]{2,1,0:T(8,128)(2,1)S(1)}, u32[]{:S(2)}, u32[]{:S(2)}) %collective-permute-start.4) | collective-permute-done | bytes 131104 | tf_op jit(solution)/shard_map/ppermute | solution.py:384
  28.9 0.0 copy-done.2
  28.9 0.0 copy-done
  28.9 0.0 copy-done.1
  28.9 2.1 %expert.1 = (f32[16,8,512]{2,1,0:T(8,128)S(1)}, bf16[16,8,512]{2,1,0:T(8,128)(2,1)S(1)}) custom-call(bf16[16,8,512]{2,1,0:T(8,128)(2,1)S(1)} %all_to_all.10.own_ref, bf16[16,8,512]{2,1,0:T(8,128)(2,1)S(1)} %collective-permute-done.4.other_ref, f32[1,4096]{1,0:T(1,128)S(1)} %get-tuple-element.45.gain_ref, bf16[4096,384]{1,0:T(8,128)(2,1)S(1)} %bitcast.10, ...), custom_call_target="tpu_custom_call" | custom-call | tf_op jit(solution)/shard_map/expert/pallas_call | solution.py:294
  31.0 0.2 collective-permute-start.5
  31.2 1.2 %collective-permute-done.5.got_ref = bf16[16,8,512]{2,1,0:T(8,128)(2,1)S(1)} collective-permute-done((bf16[16,8,512]{2,1,0:T(8,128)(2,1)S(1)}, bf16[16,8,512]{2,1,0:T(8,128)(2,1)S(1)}, u32[]{:S(2)}, u32[]{:S(2)}) %collective-permute-start.5) | collective-permute-done | bytes 131104 | tf_op jit(solution)/shard_map/ppermute | solution.py:384
  32.5 10.7 %all_to_all.11 = bf16[16,8,512]{2,1,0:T(8,128)(2,1)S(1)} all-to-all(bf16[16,8,512]{2,1,0:T(8,128)(2,1)S(1)} %merge.1), channel_id=1, replica_groups=mesh['req'=4,'head'=2,'exp'=4] {'req','exp'}, dimensions={0} | all-to-all | bytes 262144 | tf_op jit(solution)/shard_map/all_to_all | solution.py:406
  43.2 0.1 combine.1.own_ref
  43.3 0.0 collective-permute-start.6
  43.3 1.2 %collective-permute-done.6.other_ref = bf16[16,512]{1,0:T(8,128)(2,1)S(1)} collective-permute-done((bf16[16,512]{1,0:T(8,128)(2,1)S(1)}, bf16[16,512]{1,0:T(8,128)(2,1)S(1)}, u32[]{:S(2)}, u32[]{:S(2)}) %collective-permute-start.6) | collective-permute-done | bytes 16416 | tf_op jit(solution)/shard_map/ppermute | solution.py:384
  44.5 0.6 %join.1 = bf16[16,1024]{1,0:T(8,128)(2,1)} custom-call(bf16[16,512]{1,0:T(8,128)(2,1)S(1)} %combine.1.own_ref, bf16[16,512]{1,0:T(8,128)(2,1)S(1)} %collective-permute-done.6.other_ref), custom_call_target="tpu_custom_call" | custom-call | tf_op jit(solution)/shard_map/join/pallas_call | solution.py:352
  (1 shorter events, 0.0 us)
Async XLA Ops:
  2.7 7.4 %collective-permute-start.2 = (bf16[4,4096]{1,0:T(4,128)(2,1)S(1)}, bf16[4,4096]{1,0:T(4,128)(2,1)S(1)}, u32[]{:S(2)}, u32[]{:S(2)}) collective-permute-start(bf16[4,4096]{1,0:T(4,128)(2,1)S(1)} %get-tuple-element.34.refs_0_), channel_id=1, source_target_pairs={{0,3},{1,2},{2,1},{3,0},{4,7},{5,6},{6,5},{7,4},{8,11},{9,10},{10,... | collective-permute-start | bytes 98312 | tf_op jit(solution)/shard_map/ppermute | solution.py:390
  6.7 3.9 %collective-permute-start.1 = (bf16[4,4096]{1,0:T(4,128)(2,1)S(1)}, bf16[4,4096]{1,0:T(4,128)(2,1)S(1)}, u32[]{:S(2)}, u32[]{:S(2)}) collective-permute-start(bf16[4,4096]{1,0:T(4,128)(2,1)S(1)} %get-tuple-element.34.refs_0_), channel_id=1, source_target_pairs={{0,2},{1,3},{2,0},{3,1},{4,6},{5,7},{6,4},{7,5},{8,10},{9,11},{10,... | collective-permute-start | bytes 98312 | tf_op jit(solution)/shard_map/ppermute | solution.py:390
  7.2 3.9 %collective-permute-start = (bf16[4,4096]{1,0:T(4,128)(2,1)S(1)}, bf16[4,4096]{1,0:T(4,128)(2,1)S(1)}, u32[]{:S(2)}, u32[]{:S(2)}) collective-permute-start(bf16[4,4096]{1,0:T(4,128)(2,1)S(1)} %get-tuple-element.34.refs_0_), channel_id=1, source_target_pairs={{0,1},{1,0},{2,3},{3,2},{4,5},{5,4},{6,7},{7,6},{8,9},{9,8},{10,11... | collective-permute-start | bytes 98312 | tf_op jit(solution)/shard_map/ppermute | solution.py:390
  7.3 21.6 %copy-start.2 = (bf16[1,384,4096]{2,1,0:T(8,128)(2,1)S(1)}, bf16[1,384,4096]{2,1,0:T(8,128)(2,1)}, u32[]{:S(2)}) copy-start(bf16[1,384,4096]{2,1,0:T(8,128)(2,1)} %param.23) | copy-start | bytes 9437188
  11.1 17.8 %copy-start = (bf16[1,4096,384]{2,1,0:T(8,128)(2,1)S(1)}, bf16[1,4096,384]{2,1,0:T(8,128)(2,1)}, u32[]{:S(2)}) copy-start(bf16[1,4096,384]{2,1,0:T(8,128)(2,1)} %param.21) | copy-start | bytes 9437188
  11.1 17.8 %copy-start.1 = (bf16[1,4096,384]{2,1,0:T(8,128)(2,1)S(1)}, bf16[1,4096,384]{2,1,0:T(8,128)(2,1)}, u32[]{:S(2)}) copy-start(bf16[1,4096,384]{2,1,0:T(8,128)(2,1)} %param.22) | copy-start | bytes 9437188
  12.3 1.2 %collective-permute-start.3 = (f32[16,512]{1,0:T(8,128)S(1)}, f32[16,512]{1,0:T(8,128)S(1)}, u32[]{:S(2)}, u32[]{:S(2)}) collective-permute-start(f32[16,512]{1,0:T(8,128)S(1)} %get-tuple-element.41), channel_id=1, source_target_pairs={{0,4},{4,0},{1,5},{5,1},{2,6},{6,2},{3,7},{7,3},{8,12},{12,8},{9,1... | collective-permute-start | bytes 98312 | tf_op jit(solution)/shard_map/ppermute | solution.py:384
  27.5 1.3 %collective-permute-start.4 = (bf16[16,8,512]{2,1,0:T(8,128)(2,1)S(1)}, bf16[16,8,512]{2,1,0:T(8,128)(2,1)S(1)}, u32[]{:S(2)}, u32[]{:S(2)}) collective-permute-start(bf16[16,8,512]{2,1,0:T(8,128)(2,1)S(1)} %all_to_all.10.own_ref), channel_id=1, source_target_pairs={{0,4},{4,0},{1,5},{5,1},{2,6},{6,2},{3,7},{7,3},{8,12},{12,8},{9,1... | collective-permute-start | bytes 393224 | tf_op jit(solution)/shard_map/ppermute | solution.py:384
  31.0 1.4 %collective-permute-start.5 = (bf16[16,8,512]{2,1,0:T(8,128)(2,1)S(1)}, bf16[16,8,512]{2,1,0:T(8,128)(2,1)S(1)}, u32[]{:S(2)}, u32[]{:S(2)}) collective-permute-start(bf16[16,8,512]{2,1,0:T(8,128)(2,1)S(1)} %get-tuple-element.47), channel_id=1, source_target_pairs={{0,4},{4,0},{1,5},{5,1},{2,6},{6,2},{3,7},{7,3},{8,12},{12,8},{9,1... | collective-permute-start | bytes 393224 | tf_op jit(solution)/shard_map/ppermute | solution.py:384
  43.3 1.2 %collective-permute-start.6 = (bf16[16,512]{1,0:T(8,128)(2,1)S(1)}, bf16[16,512]{1,0:T(8,128)(2,1)S(1)}, u32[]{:S(2)}, u32[]{:S(2)}) collective-permute-start(bf16[16,512]{1,0:T(8,128)(2,1)S(1)} %combine.1.own_ref), channel_id=1, source_target_pairs={{0,4},{4,0},{1,5},{5,1},{2,6},{6,2},{3,7},{7,3},{8,12},{12,8},{9,1... | collective-permute-start | bytes 49160 | tf_op jit(solution)/shard_map/ppermute | solution.py:384

commit v5 on v4

--- a/solution.py
+++ b/solution.py
@@ -22,6 +22,10 @@
 
 def far(x):
     return pltpu.with_memory_space_constraint(x, pltpu.HBM)
+
+
+def side(index, span, which):
+    return pl.ds(pl.multiple_of((2 * index + which) * span, span), span)
 
 
 def attend_kernel(
@@ -187,8 +191,7 @@
 
 def project_kernel(*refs, pieces):
     parts = refs[:pieces]
-    first_ref, second_ref, keep_ref, give_ref = refs[pieces:]
-    early = first_ref.shape[0]
+    first_ref, second_ref, x_ref, give_ref = refs[pieces:]
     loaded = [p[...].astype(F32) for p in parts]
     if pieces > 1:
         place = lax.axis_index("exp")
@@ -201,21 +204,39 @@
         x = jnp.concatenate(blocks, axis=0)
     else:
         x = loaded[0]
-    x = x.astype(BF16)
-    res = jnp.dot(x[:, :early], first_ref[...], preferred_element_type=F32) + jnp.dot(
-        x[:, early:], second_ref[...], preferred_element_type=F32
-    )
-    half = keep_ref.shape[1]
-    low = lax.axis_index("head") == 0
-    keep_ref[...] = jnp.where(low, res[:, :half], res[:, half:])
-    give_ref[...] = jnp.where(low, res[:, half:], res[:, :half])
+    x_ref[...] = x.astype(BF16)
+    half_product(x_ref, first_ref, second_ref, give_ref, 1 - lax.axis_index("head"))
+
+
+def half_product(x_ref, first_ref, second_ref, o_ref, which):
+    early = first_ref.shape[0]
+    cut = side(0, o_ref.shape[1], which)
+    o_ref[...] = jnp.dot(x_ref[:, :early], first_ref[:, cut], preferred_element_type=F32) + jnp.dot(
+        x_ref[:, early:], second_ref[:, cut], preferred_element_type=F32
+    )
+
+
+def keep_kernel(x_ref, first_ref, second_ref, o_ref):
+    half_product(x_ref, first_ref, second_ref, o_ref, lax.axis_index("head"))
+
+
+def keep_half(x, first, second):
+    return pl.pallas_call(
+        keep_kernel,
+        out_shape=pltpu.VMEM((x.shape[0], first.shape[1] // 2), F32),
+        in_specs=[whole()] * 3,
+        out_specs=whole(),
+        compiler_params=pltpu.CompilerParams(vmem_limit_bytes=8 * 2**20),
+        name="keep_half",
+    )(near(x), near(first), near(second))
 
 
 def project(parts, first, second, rows):
     half = first.shape[1] // 2
+    depth = first.shape[0] + second.shape[0]
     return pl.pallas_call(
         functools.partial(project_kernel, pieces=len(parts)),
-        out_shape=(pltpu.VMEM((rows, half), F32),) * 2,
+        out_shape=(pltpu.VMEM((rows, depth), BF16), pltpu.VMEM((rows, half), F32)),
         in_specs=[whole()] * (len(parts) + 2),
         out_specs=(whole(), whole()),
         compiler_params=pltpu.CompilerParams(vmem_limit_bytes=8 * 2**20),
@@ -246,59 +267,89 @@
     )(near(own), near(other), near(resid), near(selector))
 
 
-def expert_kernel(
-    own_ref, other_ref, gain_ref, wg_ref, wu_ref, wd_ref, keep_ref, give_ref, *, groups, cols
-):
-    items, half = own_ref.shape[1:]
-    depth = 2 * cols * half
-    hid = wd_ref.shape[0]
-    low = lax.axis_index("head") == 0
-
-    def column(e, lower):
-        picks = []
-        for s in range(groups):
-            a = own_ref[s * cols + e].astype(F32)
-            b = other_ref[s * cols + e].astype(F32)
-            picks.append(jnp.where(low, a, b) if lower else jnp.where(low, b, a))
-        return jnp.concatenate(picks, axis=0)
-
-    squares = None
-    for e in range(cols):
-        for lower in (True, False):
-            x = column(e, lower)
-            part = jnp.sum(x * x, axis=1, keepdims=True)
-            squares = part if squares is None else squares + part
-    inverse = lax.rsqrt(squares / depth + 1e-06)
+def part_product(x_ref, gain_ref, wg_ref, wu_ref, groups, cols, which):
+    half = x_ref.shape[2]
+    fold = None
     acc = None
     for e in range(cols):
-        for i, lower in enumerate((True, False)):
-            sl = slice((2 * e + i) * half, (2 * e + i + 1) * half)
-            normed = (column(e, lower) * inverse * gain_ref[:, sl]).astype(BF16)
-            both = jnp.concatenate([wg_ref[sl, :], wu_ref[sl, :]], axis=1)
-            part = jnp.dot(normed, both, preferred_element_type=F32)
-            acc = part if acc is None else acc + part
+        at = side(e, half, which)
+        x = jnp.concatenate([x_ref[s * cols + e].astype(F32) for s in range(groups)], axis=0)
+        for i in range(half // 128):
+            cut = x[:, i * 128 : (i + 1) * 128]
+            fold = cut * cut if fold is None else fold + cut * cut
+        scaled = (x * gain_ref[:, at]).astype(BF16)
+        both = jnp.concatenate([wg_ref[at, :], wu_ref[at, :]], axis=1)
+        part = jnp.dot(scaled, both, preferred_element_type=F32)
+        acc = part if acc is None else acc + part
+    return acc, fold
+
+
+def first_kernel(x_ref, gain_ref, wg_ref, wu_ref, wd_ref, acc_ref, fold_ref, *, groups, cols):
+    head = lax.axis_index("head")
+    acc_ref[...], fold_ref[...] = part_product(x_ref, gain_ref, wg_ref, wu_ref, groups, cols, head)
+
+
+def expert_first(own, gain, w_gate, w_up, w_down, groups, cols):
+    rows = groups * own.shape[1]
+    return pl.pallas_call(
+        functools.partial(first_kernel, groups=groups, cols=cols),
+        out_shape=(pltpu.VMEM((rows, 2 * w_gate.shape[1]), F32), pltpu.VMEM((rows, 128), F32)),
+        in_specs=[whole()] * 5,
+        out_specs=(whole(), whole()),
+        compiler_params=pltpu.CompilerParams(vmem_limit_bytes=8 * 2**20),
+        name="expert_first",
+    )(*map(near, (own, gain, w_gate, w_up, w_down)))
+
+
+def half_down(act_ref, wd_ref, o_ref, groups, cols, which):
+    items, half = o_ref.shape[1:]
+    for e in range(cols):
+        y = jnp.dot(act_ref[...], wd_ref[:, side(e, half, which)], preferred_element_type=F32)
+        y = y.astype(o_ref.dtype)
+        for s in range(groups):
+            o_ref[s * cols + e] = y[s * items : (s + 1) * items, :]
+
+
+def second_kernel(
+    x_ref, acc_ref, fold_ref, gain_ref, wg_ref, wu_ref, wd_ref, act_ref, give_ref, *, groups, cols
+):
+    depth, hid = wg_ref.shape
+    other = 1 - lax.axis_index("head")
+    acc, fold = part_product(x_ref, gain_ref, wg_ref, wu_ref, groups, cols, other)
+    squares = jnp.sum(fold + fold_ref[...], axis=1, keepdims=True)
+    acc = (acc + acc_ref[...]) * lax.rsqrt(squares / depth + 1e-06)
     gate, up = acc[:, :hid], acc[:, hid:]
-    activated = (gate / (1.0 + jnp.exp(-gate)) * up).astype(BF16)
-    for e in range(cols):
-        y = jnp.dot(
-            activated, wd_ref[:, 2 * e * half : 2 * (e + 1) * half], preferred_element_type=F32
-        )
-        keep = jnp.where(low, y[:, :half], y[:, half:])
-        give = jnp.where(low, y[:, half:], y[:, :half]).astype(BF16)
-        for s in range(groups):
-            keep_ref[s * cols + e] = keep[s * items : (s + 1) * items, :]
-            give_ref[s * cols + e] = give[s * items : (s + 1) * items, :]
-
-
-def expert(own, other, gain, w_gate, w_up, w_down, groups, cols):
-    return pl.pallas_call(
-        functools.partial(expert_kernel, groups=groups, cols=cols),
-        out_shape=(pltpu.VMEM(own.shape, F32), pltpu.VMEM(own.shape, BF16)),
-        in_specs=[whole()] * 6,
+    act_ref[...] = (gate / (1.0 + jnp.exp(-gate)) * up).astype(BF16)
+    half_down(act_ref, wd_ref, give_ref, groups, cols, other)
+
+
+def expert_second(other, acc, fold, gain, w_gate, w_up, w_down, groups, cols):
+    return pl.pallas_call(
+        functools.partial(second_kernel, groups=groups, cols=cols),
+        out_shape=(
+            pltpu.VMEM((acc.shape[0], w_gate.shape[1]), BF16),
+            pltpu.VMEM(other.shape, BF16),
+        ),
+        in_specs=[whole()] * 7,
         out_specs=(whole(), whole()),
-        compiler_params=pltpu.CompilerParams(vmem_limit_bytes=12 * 2**20),
-        name="expert",
-    )(*map(near, (own, other, gain, w_gate, w_up, w_down)))
+        compiler_params=pltpu.CompilerParams(vmem_limit_bytes=8 * 2**20),
+        name="expert_second",
+    )(*map(near, (other, acc, fold, gain, w_gate, w_up, w_down)))
+
+
+def third_kernel(act_ref, wd_ref, keep_ref, *, groups, cols):
+    half_down(act_ref, wd_ref, keep_ref, groups, cols, lax.axis_index("head"))
+
+
+def expert_third(activated, w_down, shape, groups, cols):
+    return pl.pallas_call(
+        functools.partial(third_kernel, groups=groups, cols=cols),
+        out_shape=pltpu.VMEM(shape, F32),
+        in_specs=[whole()] * 2,
+        out_specs=whole(),
+        compiler_params=pltpu.CompilerParams(vmem_limit_bytes=8 * 2**20),
+        name="expert_third",
+    )(near(activated), near(w_down))
 
 
 def merge_kernel(keep_ref, got_ref, o_ref):
@@ -398,18 +449,26 @@
     )
     parts, staged = lax.optimization_barrier((parts, staged))
     selector, spread, near_resid, near_gain, second = staged
-    keep, give = project(parts, first, second, group_rows)
-    hidden, outgoing = dispatch(keep, swap(give), near_resid, selector)
+    joined, give = project(parts, first, second, group_rows)
+    got, keep = lax.optimization_barrier((swap(give), keep_half(joined, first, second)))
+    hidden, outgoing = dispatch(keep, got, near_resid, selector)
     half = hidden.shape[1]
+    sizes = (req_count, exp_count)
 
     def exchange(x):
         return lax.all_to_all(x, ("req", "exp"), split_axis=0, concat_axis=0, tiled=True)
 
     arrived = exchange(outgoing.reshape(expert_total, capacity, half))
-    keep, give = expert(
-        arrived, swap(arrived), near_gain, w_gate[0], w_up[0], w_down[0], req_count, exp_count
-    )
-    returned = exchange(merge(keep, swap(give)))
+    other, begun = lax.optimization_barrier(
+        (swap(arrived), expert_first(arrived, near_gain, w_gate[0], w_up[0], w_down[0], *sizes))
+    )
+    activated, give = expert_second(
+        other, *begun, near_gain, w_gate[0], w_up[0], w_down[0], *sizes
+    )
+    got, keep = lax.optimization_barrier(
+        (swap(give), expert_third(activated, w_down[0], give.shape, *sizes))
+    )
+    returned = exchange(merge(keep, got))
     mine = combine(spread, returned.reshape(expert_total * capacity, half), hidden)
     return join(mine, swap(mine))
 

time: 45.4 us -> 43.9 us (0.967)
  waiting for transfers between devices: 6.01 us -> 4.46 us
    ppermute x4, waiting for transfers between devices: 4.96 us -> 3.26 us  [swap(): return lax.ppermute(x, 'head', [(0, 1), (1, 0)])]
    pallas_call x1 -> x4, Pallas kernels: 2.14 us -> 2.81 us  [the longest x1 1.15 us: expert_second(): pl.pallas_call(functools.partial(second_kernel, groups=groups, cols=cols)...]
    pallas_call x1, Pallas kernels: 1.19 us -> 0.65 us  [project(): pl.pallas_call(functools.partial(project_kernel, pieces=len(parts)), out_...]
  transfers between devices with their start and end apart: 7 -> 7, of which waited for: 6 -> 6; matrix products, arithmetic and copies ran while one was open for 0% -> 0% of each run, Pallas kernels for 6% -> 10%
where the time goes in v5:
time: 43.9 us; the launch traced here: 43.7 us
  blocking collectives  24.7 us (56%)
  Pallas kernels  9.62 us (22%)
  starting transfers between devices  4.83 us (11%)
  waiting for transfers between devices  4.46 us (10%)
    all_to_all x2, blocking collectives, exchange(): lax.all_to_all(x, ('req', 'exp'), split_axis=0, concat_axis=0, tiled=True)  24.7 us
    ppermute x3, starting transfers between devices, local(): lax.ppermute(attended, 'exp', [(i, i ^ k) for i in range(exp_count)])  4.63 us
    ppermute x4, waiting for transfers between devices, swap(): return lax.ppermute(x, 'head', [(0, 1), (1, 0)])  3.26 us
    pallas_call x1, Pallas kernels, attend(): pl.pallas_call(functools.partial(attend_kernel, kv_heads=kv_heads), out_s...  2.65 us
    pallas_call x1, Pallas kernels, stage(): pl.pallas_call(functools.partial(stage_kernel, capacity=capacity), out_sh...  2.56 us
    ppermute x3, waiting for transfers between devices, local(): lax.ppermute(attended, 'exp', [(i, i ^ k) for i in range(exp_count)])  1.2 us
    pallas_call x1, Pallas kernels, expert_second(): pl.pallas_call(functools.partial(second_kernel, groups=groups, cols=cols)...  1.15 us
  transfers between devices with their start and end apart: 7, of which 6 were waited for; matrix products, arithmetic and copies ran while one was open for 0% of the time, Pallas kernels for 10%

profile of v5, /device:TPU:0, one launch (start us, length us, event | category | flops | bytes accessed | tf_op | source)
XLA Modules:
  0.0 43.7 jit_solution(9366394617406132311)
XLA Ops:
  0.0 2.7 %attend.1 = (bf16[4,4096]{1,0:T(4,128)(2,1)S(1)}, bf16[1536,1024]{1,0:T(8,128)(2,1)S(1)}) custom-call(s32[4]{0:T(128)} %len_hbm.1, bf16[4,32,128]{2,1,0:T(8,128)(2,1)} %q_hbm.1, bf16[4,1024,128]{2,1,0:T(8,128)(2,1)} %bitcast.19, bf16[4,1024,128]{2,1,0:T(8,128)(2,1)} %bitcast.20, bf16[4096,1024]{1,0:T(8,128)(2,1)} %w_hbm.3), custom_call_target="tpu_custom_call" | custom-call | tf_op jit(solution)/shard_map/attend/pallas_call | solution.py:104
  2.7 4.0 %collective-permute-start.2 = (bf16[4,4096]{1,0:T(4,128)(2,1)S(1)}, bf16[4,4096]{1,0:T(4,128)(2,1)S(1)}, u32[]{:S(2)}, u32[]{:S(2)}) collective-permute-start(bf16[4,4096]{1,0:T(4,128)(2,1)S(1)} %get-tuple-element.43.refs_0_), channel_id=1, source_target_pairs={{0,3},{1,2},{2,1},{3,0},{4,7},{5,6},{6,5},{7,4},{8,11},{9,10},{10,... | collective-permute-start | bytes 98312 | tf_op jit(solution)/shard_map/ppermute | solution.py:441
  6.7 0.5 %collective-permute-start.1 = (bf16[4,4096]{1,0:T(4,128)(2,1)S(1)}, bf16[4,4096]{1,0:T(4,128)(2,1)S(1)}, u32[]{:S(2)}, u32[]{:S(2)}) collective-permute-start(bf16[4,4096]{1,0:T(4,128)(2,1)S(1)} %get-tuple-element.43.refs_0_), channel_id=1, source_target_pairs={{0,2},{1,3},{2,0},{3,1},{4,6},{5,7},{6,4},{7,5},{8,10},{9,11},{10,... | collective-permute-start | bytes 98312 | tf_op jit(solution)/shard_map/ppermute | solution.py:441
  7.2 0.1 collective-permute-start
  7.3 2.6 %stage.1 = (bf16[128,16]{1,0:T(8,128)(2,1)S(1)}, f32[16,128]{1,0:T(8,128)S(1)}, bf16[16,1024]{1,0:T(8,128)(2,1)S(1)}, f32[1,4096]{1,0:T(1,128)S(1)}, bf16[2560,1024]{1,0:T(8,128)(2,1)S(1)}) custom-call(s32[8,16]{1,0:T(8,128)} %bitcast.22, f32[8,16]{1,0:T(8,128)} %bitcast.23, bf16[16,1024]{1,0:T(8,128)(2,1)} %resid_hbm.1, f32[1,4096]{1,0:T(1,128)} %bitcast.21, ...), custom_call_target="tpu_custom_call" | custom-call | tf_op jit(solution)/shard_map/stage/pallas_call | solution.py:171
  9.9 0.0 collective-permute-done.2.refs_3_
  9.9 0.7 %collective-permute-done.1.refs_2_ = bf16[4,4096]{1,0:T(4,128)(2,1)S(1)} collective-permute-done((bf16[4,4096]{1,0:T(4,128)(2,1)S(1)}, bf16[4,4096]{1,0:T(4,128)(2,1)S(1)}, u32[]{:S(2)}, u32[]{:S(2)}) %collective-permute-start.1) | collective-permute-done | bytes 32800 | tf_op jit(solution)/shard_map/ppermute | solution.py:441
  10.6 0.5 %collective-permute-done.refs_1_ = bf16[4,4096]{1,0:T(4,128)(2,1)S(1)} collective-permute-done((bf16[4,4096]{1,0:T(4,128)(2,1)S(1)}, bf16[4,4096]{1,0:T(4,128)(2,1)S(1)}, u32[]{:S(2)}, u32[]{:S(2)}) %collective-permute-start) | collective-permute-done | bytes 32800 | tf_op jit(solution)/shard_map/ppermute | solution.py:441
  11.1 0.0 copy-start.2
  11.1 0.6 %project.1 = (bf16[16,4096]{1,0:T(8,128)(2,1)S(1)}, f32[16,512]{1,0:T(8,128)S(1)}) custom-call(bf16[4,4096]{1,0:T(4,128)(2,1)S(1)} %get-tuple-element.43.refs_0_, bf16[4,4096]{1,0:T(4,128)(2,1)S(1)} %collective-permute-done.refs_1_, bf16[4,4096]{1,0:T(4,128)(2,1)S(1)} %collective-permute-done.1.refs_2_, bf16[4,4096]{1,0:T(4,128)(2,1)S(1)} %collective-permute-done.2.refs_3_, ...), custom_call_target="tpu_custom_call" | custom-call | tf_op jit(solution)/shard_map/project/pallas_call | solution.py:237
  11.7 0.0 collective-permute-start.3
  11.7 0.0 copy-start
  11.7 0.0 copy-start.1
  11.7 0.7 %keep_half.1.own_ref = f32[16,512]{1,0:T(8,128)S(1)} custom-call(bf16[16,4096]{1,0:T(8,128)(2,1)S(1)} %get-tuple-element.50.x_ref, bf16[1536,1024]{1,0:T(8,128)(2,1)S(1)} %get-tuple-element.47.refs_4_.first_ref, bf16[2560,1024]{1,0:T(8,128)(2,1)S(1)} %get-tuple-element.48.refs_5_.second_ref), custom_call_target="tpu_custom_call" | custom-call | tf_op jit(solution)/shard_map/keep_half/pallas_call | solution.py:224
  12.4 0.5 %collective-permute-done.3.other_ref = f32[16,512]{1,0:T(8,128)S(1)} collective-permute-done((f32[16,512]{1,0:T(8,128)S(1)}, f32[16,512]{1,0:T(8,128)S(1)}, u32[]{:S(2)}, u32[]{:S(2)}) %collective-permute-start.3) | collective-permute-done | bytes 32800 | tf_op jit(solution)/shard_map/ppermute | solution.py:435
  12.9 0.2 dispatch.1
  13.1 13.9 %all_to_all.10.x_ref = bf16[16,8,512]{2,1,0:T(8,128)(2,1)S(1)} all-to-all(bf16[16,8,512]{2,1,0:T(8,128)(2,1)S(1)} %bitcast.18), channel_id=1, replica_groups=mesh['req'=4,'head'=2,'exp'=4] {'req','exp'}, dimensions={0} | all-to-all | bytes 262144 | tf_op jit(solution)/shard_map/all_to_all | solution.py:459
  27.1 0.0 collective-permute-start.4
  27.1 0.0 copy-done.2
  27.1 0.0 copy-done
  27.1 0.0 copy-done.1
  27.1 0.6 %expert_first.1 = (f32[32,768]{1,0:T(8,128)S(1)}, f32[32,128]{1,0:T(8,128)S(1)}) custom-call(bf16[16,8,512]{2,1,0:T(8,128)(2,1)S(1)} %all_to_all.10.x_ref, f32[1,4096]{1,0:T(1,128)S(1)} %get-tuple-element.56.gain_ref, bf16[4096,384]{1,0:T(8,128)(2,1)S(1)} %bitcast.13, bf16[4096,384]{1,0:T(8,128)(2,1)S(1)} %bitcast.15, bf16[384,4096]{1,0:T(8,128)(2,1)S(1)} %bitcast.10), custom_call_target="tpu_custom_call" | custom-call | tf_op jit(solution)/shard_map/expert_first/pallas_call | solution.py:294
  27.7 0.7 %collective-permute-done.4.x_ref = bf16[16,8,512]{2,1,0:T(8,128)(2,1)S(1)} collective-permute-done((bf16[16,8,512]{2,1,0:T(8,128)(2,1)S(1)}, bf16[16,8,512]{2,1,0:T(8,128)(2,1)S(1)}, u32[]{:S(2)}, u32[]{:S(2)}) %collective-permute-start.4) | collective-permute-done | bytes 131104 | tf_op jit(solution)/shard_map/ppermute | solution.py:435
  28.4 1.1 %expert_second.1 = (bf16[32,384]{1,0:T(8,128)(2,1)S(1)}, bf16[16,8,512]{2,1,0:T(8,128)(2,1)S(1)}) custom-call(bf16[16,8,512]{2,1,0:T(8,128)(2,1)S(1)} %collective-permute-done.4.x_ref, f32[32,768]{1,0:T(8,128)S(1)} %get-tuple-element.60.acc_ref, f32[32,128]{1,0:T(8,128)S(1)} %get-tuple-element.61.fold_ref, f32[1,4096]{1,0:T(1,128)S(1)} %get-tuple-element.56.gain_ref, ...), custom_call_target="tpu_custom_call" | custom-call | tf_op jit(solution)/shard_map/expert_second/pallas_call | solution.py:327
  29.6 0.2 collective-permute-start.5
  29.7 0.4 expert_third.1.keep_ref
  30.1 0.8 %collective-permute-done.5.got_ref = bf16[16,8,512]{2,1,0:T(8,128)(2,1)S(1)} collective-permute-done((bf16[16,8,512]{2,1,0:T(8,128)(2,1)S(1)}, bf16[16,8,512]{2,1,0:T(8,128)(2,1)S(1)}, u32[]{:S(2)}, u32[]{:S(2)}) %collective-permute-start.5) | collective-permute-done | bytes 131104 | tf_op jit(solution)/shard_map/ppermute | solution.py:435
  31.0 10.8 %all_to_all.11 = bf16[16,8,512]{2,1,0:T(8,128)(2,1)S(1)} all-to-all(bf16[16,8,512]{2,1,0:T(8,128)(2,1)S(1)} %merge.1), channel_id=1, replica_groups=mesh['req'=4,'head'=2,'exp'=4] {'req','exp'}, dimensions={0} | all-to-all | bytes 262144 | tf_op jit(solution)/shard_map/all_to_all | solution.py:459
  41.7 0.1 combine.1.own_ref
  41.9 0.0 collective-permute-start.6
  41.9 1.2 %collective-permute-done.6.other_ref = bf16[16,512]{1,0:T(8,128)(2,1)S(1)} collective-permute-done((bf16[16,512]{1,0:T(8,128)(2,1)S(1)}, bf16[16,512]{1,0:T(8,128)(2,1)S(1)}, u32[]{:S(2)}, u32[]{:S(2)}) %collective-permute-start.6) | collective-permute-done | bytes 16416 | tf_op jit(solution)/shard_map/ppermute | solution.py:435
  43.1 0.6 %join.1 = bf16[16,1024]{1,0:T(8,128)(2,1)} custom-call(bf16[16,512]{1,0:T(8,128)(2,1)S(1)} %combine.1.own_ref, bf16[16,512]{1,0:T(8,128)(2,1)S(1)} %collective-permute-done.6.other_ref), custom_call_target="tpu_custom_call" | custom-call | tf_op jit(solution)/shard_map/join/pallas_call | solution.py:403
  (1 shorter events, 0.0 us)
Async XLA Ops:
  2.7 7.2 %collective-permute-start.2 = (bf16[4,4096]{1,0:T(4,128)(2,1)S(1)}, bf16[4,4096]{1,0:T(4,128)(2,1)S(1)}, u32[]{:S(2)}, u32[]{:S(2)}) collective-permute-start(bf16[4,4096]{1,0:T(4,128)(2,1)S(1)} %get-tuple-element.43.refs_0_), channel_id=1, source_target_pairs={{0,3},{1,2},{2,1},{3,0},{4,7},{5,6},{6,5},{7,4},{8,11},{9,10},{10,... | collective-permute-start | bytes 98312 | tf_op jit(solution)/shard_map/ppermute | solution.py:441
  6.7 3.9 %collective-permute-start.1 = (bf16[4,4096]{1,0:T(4,128)(2,1)S(1)}, bf16[4,4096]{1,0:T(4,128)(2,1)S(1)}, u32[]{:S(2)}, u32[]{:S(2)}) collective-permute-start(bf16[4,4096]{1,0:T(4,128)(2,1)S(1)} %get-tuple-element.43.refs_0_), channel_id=1, source_target_pairs={{0,2},{1,3},{2,0},{3,1},{4,6},{5,7},{6,4},{7,5},{8,10},{9,11},{10,... | collective-permute-start | bytes 98312 | tf_op jit(solution)/shard_map/ppermute | solution.py:441
  7.2 3.9 %collective-permute-start = (bf16[4,4096]{1,0:T(4,128)(2,1)S(1)}, bf16[4,4096]{1,0:T(4,128)(2,1)S(1)}, u32[]{:S(2)}, u32[]{:S(2)}) collective-permute-start(bf16[4,4096]{1,0:T(4,128)(2,1)S(1)} %get-tuple-element.43.refs_0_), channel_id=1, source_target_pairs={{0,1},{1,0},{2,3},{3,2},{4,5},{5,4},{6,7},{7,6},{8,9},{9,8},{10,11... | collective-permute-start | bytes 98312 | tf_op jit(solution)/shard_map/ppermute | solution.py:441
  11.1 16.0 %copy-start.2 = (bf16[1,4096,384]{2,1,0:T(8,128)(2,1)S(1)}, bf16[1,4096,384]{2,1,0:T(8,128)(2,1)}, u32[]{:S(2)}) copy-start(bf16[1,4096,384]{2,1,0:T(8,128)(2,1)} %param.22) | copy-start | bytes 9437188
  11.7 1.2 %collective-permute-start.3 = (f32[16,512]{1,0:T(8,128)S(1)}, f32[16,512]{1,0:T(8,128)S(1)}, u32[]{:S(2)}, u32[]{:S(2)}) collective-permute-start(f32[16,512]{1,0:T(8,128)S(1)} %get-tuple-element.49), channel_id=1, source_target_pairs={{0,4},{4,0},{1,5},{5,1},{2,6},{6,2},{3,7},{7,3},{8,12},{12,8},{9,1... | collective-permute-start | bytes 98312 | tf_op jit(solution)/shard_map/ppermute | solution.py:435
  11.7 15.3 %copy-start = (bf16[1,384,4096]{2,1,0:T(8,128)(2,1)S(1)}, bf16[1,384,4096]{2,1,0:T(8,128)(2,1)}, u32[]{:S(2)}) copy-start(bf16[1,384,4096]{2,1,0:T(8,128)(2,1)} %param.23) | copy-start | bytes 9437188
  11.7 15.3 %copy-start.1 = (bf16[1,4096,384]{2,1,0:T(8,128)(2,1)S(1)}, bf16[1,4096,384]{2,1,0:T(8,128)(2,1)}, u32[]{:S(2)}) copy-start(bf16[1,4096,384]{2,1,0:T(8,128)(2,1)} %param.21) | copy-start | bytes 9437188
  27.1 1.3 %collective-permute-start.4 = (bf16[16,8,512]{2,1,0:T(8,128)(2,1)S(1)}, bf16[16,8,512]{2,1,0:T(8,128)(2,1)S(1)}, u32[]{:S(2)}, u32[]{:S(2)}) collective-permute-start(bf16[16,8,512]{2,1,0:T(8,128)(2,1)S(1)} %all_to_all.10.x_ref), channel_id=1, source_target_pairs={{0,4},{4,0},{1,5},{5,1},{2,6},{6,2},{3,7},{7,3},{8,12},{12,8},{9,1... | collective-permute-start | bytes 393224 | tf_op jit(solution)/shard_map/ppermute | solution.py:435
  29.6 1.4 %collective-permute-start.5 = (bf16[16,8,512]{2,1,0:T(8,128)(2,1)S(1)}, bf16[16,8,512]{2,1,0:T(8,128)(2,1)S(1)}, u32[]{:S(2)}, u32[]{:S(2)}) collective-permute-start(bf16[16,8,512]{2,1,0:T(8,128)(2,1)S(1)} %get-tuple-element.62), channel_id=1, source_target_pairs={{0,4},{4,0},{1,5},{5,1},{2,6},{6,2},{3,7},{7,3},{8,12},{12,8},{9,1... | collective-permute-start | bytes 393224 | tf_op jit(solution)/shard_map/ppermute | solution.py:435
  41.9 1.2 %collective-permute-start.6 = (bf16[16,512]{1,0:T(8,128)(2,1)S(1)}, bf16[16,512]{1,0:T(8,128)(2,1)S(1)}, u32[]{:S(2)}, u32[]{:S(2)}) collective-permute-start(bf16[16,512]{1,0:T(8,128)(2,1)S(1)} %combine.1.own_ref), channel_id=1, source_target_pairs={{0,4},{4,0},{1,5},{5,1},{2,6},{6,2},{3,7},{7,3},{8,12},{12,8},{9,1... | collective-permute-start | bytes 49160 | tf_op jit(solution)/shard_map/ppermute | solution.py:435

commit v6 on v5

--- a/solution.py
+++ b/solution.py
@@ -29,8 +29,7 @@
 
 
 def attend_kernel(
-    len_hbm, q_hbm, k_hbm, v_hbm, w_hbm, o_ref, w_ref, len_ref, q_ref, kbuf, vbuf, scr, sems, one,
-    *, kv_heads
+    len_hbm, q_hbm, k_hbm, v_hbm, o_ref, len_ref, q_ref, kbuf, vbuf, scr, sems, one, *, kv_heads
 ):
     rows, heads, size = q_ref.shape
     width = kbuf.shape[1]
@@ -39,10 +38,9 @@
     tiles = width // tile
     ask = pltpu.make_async_copy(q_hbm, q_ref, one.at[0])
     span = pltpu.make_async_copy(len_hbm, len_ref, one.at[1])
-    load = pltpu.make_async_copy(w_hbm.at[pl.ds(0, w_ref.shape[0])], w_ref, one.at[2])
-    kcs = [pltpu.make_async_copy(k_hbm.at[t], kbuf.at[t], sems.at[0, t]) for t in range(rows)]
-    vcs = [pltpu.make_async_copy(v_hbm.at[t], vbuf.at[t], sems.at[1, t]) for t in range(rows)]
-    for c in [ask, span] + kcs + vcs + [load]:
+    kcs = [pltpu.make_async_copy(k_hbm, kbuf, sems.at[0, 0])]
+    vcs = [pltpu.make_async_copy(v_hbm, vbuf, sems.at[1, 0])]
+    for c in [ask, span] + kcs + vcs:
         c.start()
     lane = lax.broadcasted_iota(jnp.int32, (per, tile), 1)
     group = lane % kv_heads
@@ -94,21 +92,17 @@
         )
     for j in range(heads):
         o_ref[:, j * size : (j + 1) * size] = scr[pl.ds(j, rows, stride=heads), :].astype(BF16)
-    load.wait()
-
-
-def attend(queries, keys, values, lengths, out_weight, early):
+
+
+def attend(queries, keys, values, lengths):
     rows, heads, size = queries.shape
     slots, kv_heads = keys.shape[1:3]
     flat = (rows, slots * kv_heads, size)
     return pl.pallas_call(
         functools.partial(attend_kernel, kv_heads=kv_heads),
-        out_shape=(
-            pltpu.VMEM((rows, heads * size), BF16),
-            pltpu.VMEM((early, out_weight.shape[1]), BF16),
-        ),
-        in_specs=[whole(pltpu.HBM)] * 5,
-        out_specs=(whole(), whole()),
+        out_shape=pltpu.VMEM((rows, heads * size), BF16),
+        in_specs=[whole(pltpu.HBM)] * 4,
+        out_specs=whole(),
         scratch_shapes=[
             pltpu.SMEM((rows,), jnp.int32),
             pltpu.VMEM(queries.shape, BF16),
@@ -116,33 +110,16 @@
             pltpu.VMEM(flat, BF16),
             pltpu.VMEM((rows * heads, size), F32),
             pltpu.SemaphoreType.DMA((2, rows)),
-            pltpu.SemaphoreType.DMA((3,)),
+            pltpu.SemaphoreType.DMA((2,)),
         ],
         compiler_params=pltpu.CompilerParams(vmem_limit_bytes=8 * 2**20),
         name="attend",
-    )(*map(far, (lengths, queries, keys.reshape(flat), values.reshape(flat), out_weight)))
-
-
-def stage_kernel(
-    ids_hbm, weight_hbm, resid_hbm, gain_hbm, w_hbm,
-    sel_ref, spread_ref, resid_ref, gain_ref, w_ref, ids_ref, weight_ref, sems,
-    *, capacity,
-):
-    tail = w_hbm.at[pl.ds(w_hbm.shape[0] - w_ref.shape[0], w_ref.shape[0])]
-    pairs = (
-        (ids_hbm, ids_ref),
-        (weight_hbm, weight_ref),
-        (tail, w_ref),
-        (resid_hbm, resid_ref),
-        (gain_hbm, gain_ref),
-    )
-    loads = [pltpu.make_async_copy(a, b, sems.at[i]) for i, (a, b) in enumerate(pairs)]
-    for c in loads:
-        c.start()
+    )(*map(far, (lengths, queries, keys.reshape(flat), values.reshape(flat))))
+
+
+def stage_kernel(ids_ref, weight_ref, sel_ref, spread_ref, *, capacity):
     total, rows = sel_ref.shape
     experts = total // capacity
-    loads[0].wait()
-    loads[1].wait()
     expert = lax.broadcasted_iota(jnp.int32, (experts, rows), 0)
     chosen = jnp.zeros((experts, rows), F32)
     weight = jnp.zeros((experts, rows), F32)
@@ -160,38 +137,24 @@
     shares = jnp.where(taken, jnp.broadcast_to(weight[:, None, :], seat.shape), 0.0)
     sel_ref[...] = jnp.where(taken, 1.0, 0.0).reshape(total, rows).astype(BF16)
     spread_ref[...] = shares.reshape(total, rows).T
-    for c in loads[2:]:
-        c.wait()
-
-
-def stage(expert_ids, route_weights, resid, gain, out_weight, experts, capacity, early):
-    rows, top = expert_ids.shape
+
+
+def stage(expert_ids, route_weights, experts, capacity):
+    rows = expert_ids.shape[0]
     total = experts * capacity
-    depth, width = out_weight.shape
     return pl.pallas_call(
         functools.partial(stage_kernel, capacity=capacity),
-        out_shape=(
-            pltpu.VMEM((total, rows), BF16),
-            pltpu.VMEM((rows, total), F32),
-            pltpu.VMEM(resid.shape, BF16),
-            pltpu.VMEM(gain.shape, F32),
-            pltpu.VMEM((depth - early, width), BF16),
-        ),
-        in_specs=[whole(pltpu.HBM)] * 5,
-        out_specs=(whole(),) * 5,
-        scratch_shapes=[
-            pltpu.VMEM((top, rows), jnp.int32),
-            pltpu.VMEM((top, rows), F32),
-            pltpu.SemaphoreType.DMA((5,)),
-        ],
+        out_shape=(pltpu.VMEM((total, rows), BF16), pltpu.VMEM((rows, total), F32)),
+        in_specs=[whole(), whole()],
+        out_specs=(whole(), whole()),
         compiler_params=pltpu.CompilerParams(vmem_limit_bytes=8 * 2**20),
         name="stage",
-    )(*map(far, (expert_ids.T, route_weights.T, resid, gain, out_weight)))
+    )(near(expert_ids.T), near(route_weights.T))
 
 
 def project_kernel(*refs, pieces):
     parts = refs[:pieces]
-    first_ref, second_ref, x_ref, give_ref = refs[pieces:]
+    w_ref, tail_ref, x_ref, give_ref = refs[pieces:]
     loaded = [p[...].astype(F32) for p in parts]
     if pieces > 1:
         place = lax.axis_index("exp")
@@ -205,43 +168,42 @@
     else:
         x = loaded[0]
     x_ref[...] = x.astype(BF16)
-    half_product(x_ref, first_ref, second_ref, give_ref, 1 - lax.axis_index("head"))
-
-
-def half_product(x_ref, first_ref, second_ref, o_ref, which):
-    early = first_ref.shape[0]
+    half_product(x_ref, w_ref, tail_ref, give_ref, 1 - lax.axis_index("head"))
+
+
+def half_product(x_ref, w_ref, tail_ref, o_ref, which):
     cut = side(0, o_ref.shape[1], which)
-    o_ref[...] = jnp.dot(x_ref[:, :early], first_ref[:, cut], preferred_element_type=F32) + jnp.dot(
-        x_ref[:, early:], second_ref[:, cut], preferred_element_type=F32
-    )
-
-
-def keep_kernel(x_ref, first_ref, second_ref, o_ref):
-    half_product(x_ref, first_ref, second_ref, o_ref, lax.axis_index("head"))
-
-
-def keep_half(x, first, second):
+    early = w_ref.shape[0] - tail_ref.shape[0]
+    o_ref[...] = jnp.dot(
+        x_ref[:, :early], w_ref[:early, cut], preferred_element_type=F32
+    ) + jnp.dot(x_ref[:, early:], tail_ref[:, cut], preferred_element_type=F32)
+
+
+def keep_kernel(x_ref, w_ref, tail_ref, o_ref):
+    half_product(x_ref, w_ref, tail_ref, o_ref, lax.axis_index("head"))
+
+
+def keep_half(x, out_weight, tail):
     return pl.pallas_call(
         keep_kernel,
-        out_shape=pltpu.VMEM((x.shape[0], first.shape[1] // 2), F32),
+        out_shape=pltpu.VMEM((x.shape[0], out_weight.shape[1] // 2), F32),
         in_specs=[whole()] * 3,
         out_specs=whole(),
         compiler_params=pltpu.CompilerParams(vmem_limit_bytes=8 * 2**20),
         name="keep_half",
-    )(near(x), near(first), near(second))
-
-
-def project(parts, first, second, rows):
-    half = first.shape[1] // 2
-    depth = first.shape[0] + second.shape[0]
+    )(near(x), near(out_weight), near(tail))
+
+
+def project(parts, out_weight, tail, rows):
+    depth, width = out_weight.shape
     return pl.pallas_call(
         functools.partial(project_kernel, pieces=len(parts)),
-        out_shape=(pltpu.VMEM((rows, depth), BF16), pltpu.VMEM((rows, half), F32)),
+        out_shape=(pltpu.VMEM((rows, depth), BF16), pltpu.VMEM((rows, width // 2), F32)),
         in_specs=[whole()] * (len(parts) + 2),
         out_specs=(whole(), whole()),
         compiler_params=pltpu.CompilerParams(vmem_limit_bytes=8 * 2**20),
         name="project",
-    )(*map(near, parts), near(first), near(second))
+    )(*map(near, parts), near(out_weight), near(tail))
 
 
 def dispatch_kernel(own_ref, other_ref, resid_ref, sel_ref, hid_ref, out_ref):
@@ -434,8 +396,7 @@
     def swap(x):
         return lax.ppermute(x, "head", [(0, 1), (1, 0)])
 
-    early = out_weight.shape[0] * 3 // 8
-    attended, first = attend(queries, keys, values, lengths, out_weight, early)
+    attended = attend(queries, keys, values, lengths)
     if exp_count == 4:
         parts = [attended] + [
             lax.ppermute(attended, "exp", [(i, i ^ k) for i in range(exp_count)])
@@ -444,13 +405,12 @@
     else:
         parts = [lax.all_gather(attended, "exp", axis=0, tiled=True)]
 
-    staged = stage(
-        expert_ids, route_weights, resid, norm_gain[None, :], out_weight, expert_total, capacity, early
-    )
-    parts, staged = lax.optimization_barrier((parts, staged))
-    selector, spread, near_resid, near_gain, second = staged
-    joined, give = project(parts, first, second, group_rows)
-    got, keep = lax.optimization_barrier((swap(give), keep_half(joined, first, second)))
+    selector, spread = stage(expert_ids, route_weights, expert_total, capacity)
+    parts, selector, spread = lax.optimization_barrier((parts, selector, spread))
+    tail = out_weight[out_weight.shape[0] * 5 // 8 :]
+    near_resid, near_gain = resid, norm_gain[None, :]
+    joined, give = project(parts, out_weight, tail, group_rows)
+    got, keep = lax.optimization_barrier((swap(give), keep_half(joined, out_weight, tail)))
     hidden, outgoing = dispatch(keep, got, near_resid, selector)
     half = hidden.shape[1]
     sizes = (req_count, exp_count)

time: 43.9 us -> 43.5 us (level)
  Pallas kernels: 9.62 us -> 7.01 us
  local copies, waits for them, and re-layouts: 0.02 us -> 2.25 us
    pallas_call x1, Pallas kernels: 2.56 us -> 0.19 us  [stage(): pl.pallas_call(functools.partial(stage_kernel, capacity=capacity), out_sh...]
    slice x0 -> x1, local copies, waits for them, and re-layouts: none -> 2.19 us  [local(): tail = out_weight[out_weight.shape[0] * 5 // 8:]]
  transfers between devices with their start and end apart: 7 -> 7, of which waited for: 6 -> 6; matrix products, arithmetic and copies ran while one was open for 0% -> 5% of each run, Pallas kernels for 10% -> 4%
where the time goes in v6:
time: 43.5 us; the launch traced here: 43.3 us
  blocking collectives  24.5 us (56%)
  Pallas kernels  7.01 us (16%)
  starting transfers between devices  4.83 us (11%)
  waiting for transfers between devices  4.6 us (11%)
  local copies, waits for them, and re-layouts  2.25 us (5%)
    all_to_all x2, blocking collectives, exchange(): lax.all_to_all(x, ('req', 'exp'), split_axis=0, concat_axis=0, tiled=True)  24.5 us
    ppermute x3, starting transfers between devices, local(): lax.ppermute(attended, 'exp', [(i, i ^ k) for i in range(exp_count)])  4.63 us
    ppermute x4, waiting for transfers between devices, swap(): return lax.ppermute(x, 'head', [(0, 1), (1, 0)])  3.22 us
    pallas_call x1, Pallas kernels, attend(): pl.pallas_call(functools.partial(attend_kernel, kv_heads=kv_heads), out_s...  2.43 us
    slice x1, local copies, waits for them, and re-layouts, local(): tail = out_weight[out_weight.shape[0] * 5 // 8:]  2.19 us
    ppermute x3, waiting for transfers between devices, local(): lax.ppermute(attended, 'exp', [(i, i ^ k) for i in range(exp_count)])  1.37 us
    pallas_call x1, Pallas kernels, expert_second(): pl.pallas_call(functools.partial(second_kernel, groups=groups, cols=cols)...  1.15 us
  transfers between devices with their start and end apart: 7, of which 6 were waited for; matrix products, arithmetic and copies ran while one was open for 5% of the time, Pallas kernels for 4%

profile of v6, /device:TPU:0, one launch (start us, length us, event | category | flops | bytes accessed | tf_op | source)
XLA Modules:
  0.0 43.3 jit_solution(6072258947531917700)
XLA Ops:
  0.0 2.4 %attend.1.refs_0_ = bf16[4,4096]{1,0:T(4,128)(2,1)S(1)} custom-call(s32[4]{0:T(128)} %len_hbm.1, bf16[4,32,128]{2,1,0:T(8,128)(2,1)} %q_hbm.1, bf16[4,1024,128]{2,1,0:T(8,128)(2,1)} %bitcast.23, bf16[4,1024,128]{2,1,0:T(8,128)(2,1)} %bitcast.24), custom_call_target="tpu_custom_call" | custom-call | tf_op jit(solution)/shard_map/attend/pallas_call | solution.py:101
  2.4 0.0 copy-start.6
  2.4 0.0 copy-start.7
  2.5 4.0 %collective-permute-start.2 = (bf16[4,4096]{1,0:T(4,128)(2,1)S(1)}, bf16[4,4096]{1,0:T(4,128)(2,1)S(1)}, u32[]{:S(2)}, u32[]{:S(2)}) collective-permute-start(bf16[4,4096]{1,0:T(4,128)(2,1)S(1)} %attend.1.refs_0_), channel_id=1, source_target_pairs={{0,3},{1,2},{2,1},{3,0},{4,7},{5,6},{6,5},{7,4},{8,11},{9,10},{10,... | collective-permute-start | bytes 98312 | tf_op jit(solution)/shard_map/ppermute | solution.py:402
  6.5 0.5 %collective-permute-start.1 = (bf16[4,4096]{1,0:T(4,128)(2,1)S(1)}, bf16[4,4096]{1,0:T(4,128)(2,1)S(1)}, u32[]{:S(2)}, u32[]{:S(2)}) collective-permute-start(bf16[4,4096]{1,0:T(4,128)(2,1)S(1)} %attend.1.refs_0_), channel_id=1, source_target_pairs={{0,2},{1,3},{2,0},{3,1},{4,6},{5,7},{6,4},{7,5},{8,10},{9,11},{10,... | collective-permute-start | bytes 98312 | tf_op jit(solution)/shard_map/ppermute | solution.py:402
  7.0 0.1 collective-permute-start
  7.1 2.2 %slice.3.refs_5_.tail_ref = bf16[1536,1024]{1,0:T(8,128)(2,1)S(1)} slice(bf16[4096,1024]{1,0:T(8,128)(2,1)} %w_ref.1), slice={[2560:4096], [0:1024]} | slice | bytes 6291456 | tf_op jit(solution)/shard_map/slice | solution.py:410
  9.3 0.2 stage.1
  9.5 0.0 collective-permute-done.2.refs_3_
  9.5 0.9 %collective-permute-done.1.refs_2_ = bf16[4,4096]{1,0:T(4,128)(2,1)S(1)} collective-permute-done((bf16[4,4096]{1,0:T(4,128)(2,1)S(1)}, bf16[4,4096]{1,0:T(4,128)(2,1)S(1)}, u32[]{:S(2)}, u32[]{:S(2)}) %collective-permute-start.1) | collective-permute-done | bytes 32800 | tf_op jit(solution)/shard_map/ppermute | solution.py:402
  10.4 0.5 %collective-permute-done.refs_1_ = bf16[4,4096]{1,0:T(4,128)(2,1)S(1)} collective-permute-done((bf16[4,4096]{1,0:T(4,128)(2,1)S(1)}, bf16[4,4096]{1,0:T(4,128)(2,1)S(1)}, u32[]{:S(2)}, u32[]{:S(2)}) %collective-permute-start) | collective-permute-done | bytes 32800 | tf_op jit(solution)/shard_map/ppermute | solution.py:402
  10.9 0.6 %project.1 = (bf16[16,4096]{1,0:T(8,128)(2,1)S(1)}, f32[16,512]{1,0:T(8,128)S(1)}) custom-call(bf16[4,4096]{1,0:T(4,128)(2,1)S(1)} %attend.1.refs_0_, bf16[4,4096]{1,0:T(4,128)(2,1)S(1)} %collective-permute-done.refs_1_, bf16[4,4096]{1,0:T(4,128)(2,1)S(1)} %collective-permute-done.1.refs_2_, bf16[4,4096]{1,0:T(4,128)(2,1)S(1)} %collective-permute-done.2.refs_3_, ...), custom_call_target="tpu_custom_call" | custom-call | tf_op jit(solution)/shard_map/project/pallas_call | solution.py:199
  11.5 0.0 collective-permute-start.3
  11.5 0.0 copy-start.1
  11.5 0.0 copy-start.2
  11.6 0.0 copy-start.3
  11.6 0.0 copy-start.4
  11.6 0.7 %keep_half.1.own_ref = f32[16,512]{1,0:T(8,128)S(1)} custom-call(bf16[16,4096]{1,0:T(8,128)(2,1)S(1)} %get-tuple-element.36.x_ref, bf16[4096,1024]{1,0:T(8,128)(2,1)S(1)} %copy-done, bf16[1536,1024]{1,0:T(8,128)(2,1)S(1)} %slice.3.refs_5_.tail_ref), custom_call_target="tpu_custom_call" | custom-call | tf_op jit(solution)/shard_map/keep_half/pallas_call | solution.py:187
  12.2 0.5 %collective-permute-done.3.other_ref = f32[16,512]{1,0:T(8,128)S(1)} collective-permute-done((f32[16,512]{1,0:T(8,128)S(1)}, f32[16,512]{1,0:T(8,128)S(1)}, u32[]{:S(2)}, u32[]{:S(2)}) %collective-permute-start.3) | collective-permute-done | bytes 32800 | tf_op jit(solution)/shard_map/ppermute | solution.py:397
  12.8 0.2 dispatch.1
  12.9 13.8 %all_to_all.10.x_ref = bf16[16,8,512]{2,1,0:T(8,128)(2,1)S(1)} all-to-all(bf16[16,8,512]{2,1,0:T(8,128)(2,1)S(1)} %bitcast.18), channel_id=1, replica_groups=mesh['req'=4,'head'=2,'exp'=4] {'req','exp'}, dimensions={0} | all-to-all | bytes 262144 | tf_op jit(solution)/shard_map/all_to_all | solution.py:419
  26.7 0.0 collective-permute-start.4
  26.7 0.6 %expert_first.1 = (f32[32,768]{1,0:T(8,128)S(1)}, f32[32,128]{1,0:T(8,128)S(1)}) custom-call(bf16[16,8,512]{2,1,0:T(8,128)(2,1)S(1)} %all_to_all.10.x_ref, f32[1,4096]{1,0:T(1,128)S(1)} %bitcast.19, bf16[4096,384]{1,0:T(8,128)(2,1)S(1)} %bitcast.13, bf16[4096,384]{1,0:T(8,128)(2,1)S(1)} %bitcast.15, bf16[384,4096]{1,0:T(8,128)(2,1)S(1)} %bitcast.10), custom_call_target="tpu_custom_call" | custom-call | tf_op jit(solution)/shard_map/expert_first/pallas_call | solution.py:256
  27.4 0.7 %collective-permute-done.4.x_ref = bf16[16,8,512]{2,1,0:T(8,128)(2,1)S(1)} collective-permute-done((bf16[16,8,512]{2,1,0:T(8,128)(2,1)S(1)}, bf16[16,8,512]{2,1,0:T(8,128)(2,1)S(1)}, u32[]{:S(2)}, u32[]{:S(2)}) %collective-permute-start.4) | collective-permute-done | bytes 131104 | tf_op jit(solution)/shard_map/ppermute | solution.py:397
  28.1 1.2 %expert_second.1 = (bf16[32,384]{1,0:T(8,128)(2,1)S(1)}, bf16[16,8,512]{2,1,0:T(8,128)(2,1)S(1)}) custom-call(bf16[16,8,512]{2,1,0:T(8,128)(2,1)S(1)} %collective-permute-done.4.x_ref, f32[32,768]{1,0:T(8,128)S(1)} %get-tuple-element.44.acc_ref, f32[32,128]{1,0:T(8,128)S(1)} %get-tuple-element.45.fold_ref, f32[1,4096]{1,0:T(1,128)S(1)} %bitcast.20, ...), custom_call_target="tpu_custom_call" | custom-call | tf_op jit(solution)/shard_map/expert_second/pallas_call | solution.py:289
  29.2 0.2 collective-permute-start.5
  29.4 0.4 expert_third.1.keep_ref
  29.8 0.8 %collective-permute-done.5.got_ref = bf16[16,8,512]{2,1,0:T(8,128)(2,1)S(1)} collective-permute-done((bf16[16,8,512]{2,1,0:T(8,128)(2,1)S(1)}, bf16[16,8,512]{2,1,0:T(8,128)(2,1)S(1)}, u32[]{:S(2)}, u32[]{:S(2)}) %collective-permute-start.5) | collective-permute-done | bytes 131104 | tf_op jit(solution)/shard_map/ppermute | solution.py:397
  30.6 10.7 %all_to_all.11 = bf16[16,8,512]{2,1,0:T(8,128)(2,1)S(1)} all-to-all(bf16[16,8,512]{2,1,0:T(8,128)(2,1)S(1)} %merge.1), channel_id=1, replica_groups=mesh['req'=4,'head'=2,'exp'=4] {'req','exp'}, dimensions={0} | all-to-all | bytes 262144 | tf_op jit(solution)/shard_map/all_to_all | solution.py:419
  41.4 0.1 combine.1.own_ref
  41.5 1.2 %collective-permute-done.6.other_ref = bf16[16,512]{1,0:T(8,128)(2,1)S(1)} collective-permute-done((bf16[16,512]{1,0:T(8,128)(2,1)S(1)}, bf16[16,512]{1,0:T(8,128)(2,1)S(1)}, u32[]{:S(2)}, u32[]{:S(2)}) %collective-permute-start.6) | collective-permute-done | bytes 16416 | tf_op jit(solution)/shard_map/ppermute | solution.py:397
  42.7 0.6 %join.1 = bf16[16,1024]{1,0:T(8,128)(2,1)} custom-call(bf16[16,512]{1,0:T(8,128)(2,1)S(1)} %combine.1.own_ref, bf16[16,512]{1,0:T(8,128)(2,1)S(1)} %collective-permute-done.6.other_ref), custom_call_target="tpu_custom_call" | custom-call | tf_op jit(solution)/shard_map/join/pallas_call | solution.py:365
  (12 shorter events, 0.0 us)
Async XLA Ops:
  0.0 10.9 %copy-start = (bf16[4096,1024]{1,0:T(8,128)(2,1)S(1)}, bf16[4096,1024]{1,0:T(8,128)(2,1)}, u32[]{:S(2)}) copy-start(bf16[4096,1024]{1,0:T(8,128)(2,1)} %w_ref.1) | copy-start | bytes 25165828
  2.4 6.9 %copy-start.6 = (s32[16,8]{0,1:T(8,128)S(1)}, s32[16,8]{0,1:T(8,128)}, u32[]{:S(2)}) copy-start(s32[16,8]{0,1:T(8,128)} %param.19) | copy-start | bytes 1540
  2.4 6.9 %copy-start.7 = (f32[16,8]{0,1:T(8,128)S(1)}, f32[16,8]{0,1:T(8,128)}, u32[]{:S(2)}) copy-start(f32[16,8]{0,1:T(8,128)} %param.20) | copy-start | bytes 1540
  2.5 7.0 %collective-permute-start.2 = (bf16[4,4096]{1,0:T(4,128)(2,1)S(1)}, bf16[4,4096]{1,0:T(4,128)(2,1)S(1)}, u32[]{:S(2)}, u32[]{:S(2)}) collective-permute-start(bf16[4,4096]{1,0:T(4,128)(2,1)S(1)} %attend.1.refs_0_), channel_id=1, source_target_pairs={{0,3},{1,2},{2,1},{3,0},{4,7},{5,6},{6,5},{7,4},{8,11},{9,10},{10,... | collective-permute-start | bytes 98312 | tf_op jit(solution)/shard_map/ppermute | solution.py:402
  6.5 3.9 %collective-permute-start.1 = (bf16[4,4096]{1,0:T(4,128)(2,1)S(1)}, bf16[4,4096]{1,0:T(4,128)(2,1)S(1)}, u32[]{:S(2)}, u32[]{:S(2)}) collective-permute-start(bf16[4,4096]{1,0:T(4,128)(2,1)S(1)} %attend.1.refs_0_), channel_id=1, source_target_pairs={{0,2},{1,3},{2,0},{3,1},{4,6},{5,7},{6,4},{7,5},{8,10},{9,11},{10,... | collective-permute-start | bytes 98312 | tf_op jit(solution)/shard_map/ppermute | solution.py:402
  7.0 3.9 %collective-permute-start = (bf16[4,4096]{1,0:T(4,128)(2,1)S(1)}, bf16[4,4096]{1,0:T(4,128)(2,1)S(1)}, u32[]{:S(2)}, u32[]{:S(2)}) collective-permute-start(bf16[4,4096]{1,0:T(4,128)(2,1)S(1)} %attend.1.refs_0_), channel_id=1, source_target_pairs={{0,1},{1,0},{2,3},{3,2},{4,5},{5,4},{6,7},{7,6},{8,9},{9,8},{10,11... | collective-permute-start | bytes 98312 | tf_op jit(solution)/shard_map/ppermute | solution.py:402
  11.5 1.2 %collective-permute-start.3 = (f32[16,512]{1,0:T(8,128)S(1)}, f32[16,512]{1,0:T(8,128)S(1)}, u32[]{:S(2)}, u32[]{:S(2)}) collective-permute-start(f32[16,512]{1,0:T(8,128)S(1)} %get-tuple-element.35), channel_id=1, source_target_pairs={{0,4},{4,0},{1,5},{5,1},{2,6},{6,2},{3,7},{7,3},{8,12},{12,8},{9,1... | collective-permute-start | bytes 98312 | tf_op jit(solution)/shard_map/ppermute | solution.py:397
  11.5 1.2 %copy-start.5 = (bf16[16,1024]{1,0:T(8,128)(2,1)S(1)}, bf16[16,1024]{1,0:T(8,128)(2,1)}, u32[]{:S(2)}) copy-start(bf16[16,1024]{1,0:T(8,128)(2,1)} %resid_ref.1) | copy-start | bytes 98308
  11.5 15.2 %copy-start.1 = (bf16[1,384,4096]{2,1,0:T(8,128)(2,1)S(1)}, bf16[1,384,4096]{2,1,0:T(8,128)(2,1)}, u32[]{:S(2)}) copy-start(bf16[1,384,4096]{2,1,0:T(8,128)(2,1)} %param.23) | copy-start | bytes 9437188
  11.5 15.2 %copy-start.2 = (bf16[1,4096,384]{2,1,0:T(8,128)(2,1)S(1)}, bf16[1,4096,384]{2,1,0:T(8,128)(2,1)}, u32[]{:S(2)}) copy-start(bf16[1,4096,384]{2,1,0:T(8,128)(2,1)} %param.21) | copy-start | bytes 9437188
  11.6 15.2 %copy-start.3 = (bf16[1,4096,384]{2,1,0:T(8,128)(2,1)S(1)}, bf16[1,4096,384]{2,1,0:T(8,128)(2,1)}, u32[]{:S(2)}) copy-start(bf16[1,4096,384]{2,1,0:T(8,128)(2,1)} %param.22) | copy-start | bytes 9437188
  11.6 15.2 %copy-start.4 = (f32[4096]{0:T(1024)S(1)}, f32[4096]{0:T(1024)}, u32[]{:S(2)}) copy-start(f32[4096]{0:T(1024)} %param.18) | copy-start | bytes 49156
  26.7 1.3 %collective-permute-start.4 = (bf16[16,8,512]{2,1,0:T(8,128)(2,1)S(1)}, bf16[16,8,512]{2,1,0:T(8,128)(2,1)S(1)}, u32[]{:S(2)}, u32[]{:S(2)}) collective-permute-start(bf16[16,8,512]{2,1,0:T(8,128)(2,1)S(1)} %all_to_all.10.x_ref), channel_id=1, source_target_pairs={{0,4},{4,0},{1,5},{5,1},{2,6},{6,2},{3,7},{7,3},{8,12},{12,8},{9,1... | collective-permute-start | bytes 393224 | tf_op jit(solution)/shard_map/ppermute | solution.py:397
  29.2 1.4 %collective-permute-start.5 = (bf16[16,8,512]{2,1,0:T(8,128)(2,1)S(1)}, bf16[16,8,512]{2,1,0:T(8,128)(2,1)S(1)}, u32[]{:S(2)}, u32[]{:S(2)}) collective-permute-start(bf16[16,8,512]{2,1,0:T(8,128)(2,1)S(1)} %get-tuple-element.46), channel_id=1, source_target_pairs={{0,4},{4,0},{1,5},{5,1},{2,6},{6,2},{3,7},{7,3},{8,12},{12,8},{9,1... | collective-permute-start | bytes 393224 | tf_op jit(solution)/shard_map/ppermute | solution.py:397
  41.5 1.2 %collective-permute-start.6 = (bf16[16,512]{1,0:T(8,128)(2,1)S(1)}, bf16[16,512]{1,0:T(8,128)(2,1)S(1)}, u32[]{:S(2)}, u32[]{:S(2)}) collective-permute-start(bf16[16,512]{1,0:T(8,128)(2,1)S(1)} %combine.1.own_ref), channel_id=1, source_target_pairs={{0,4},{4,0},{1,5},{5,1},{2,6},{6,2},{3,7},{7,3},{8,12},{12,8},{9,1... | collective-permute-start | bytes 49160 | tf_op jit(solution)/shard_map/ppermute | solution.py:397
